TPU v7x, 32 devices: a whole 2x2x4 slice. The times are simulated.
32 devices in a mesh: row: 4 (over y, x), col: 8 (over z, core).
Axes of the slice: x: 2, y: 2, z: 4, core: 2. Of those that a mesh axis runs over, the one named last changes fastest.
Arguments:
- covariance: float32 [6144, 6144], P(('row', 'col')), may hold values from -1 to 10, as said below
- advective_ratio: float32 [1, 4, 2, 6144], P(None, None, None, ('row', 'col')), may hold values from 0.05 to 0.45
- flow_heading_flags: int32 [1, 4, 2, 6144], replicated, may hold values 0 or 1
- cell_of_state: int32 [6144], replicated, may hold values from 0 to 6143, as said below
- added_uncertainty: float32 [1, 6144], P(None, ('row', 'col')), may hold values from 0.2 to 1
Outputs:
- forecast_cov: float32 [6144, 6144], P(('row', 'col'))
Inputs may be any that keep to these rules, and one draw needn't show every extreme that they name: covariance is exactly symmetric. cell_of_state names every grid cell exactly once.
All inputs are finite; a program needn't handle non-finite values.
Results may differ from a plain program's by a relative error of at most 0.00002.
Values sent between devices are 32-bit elements; how exact they have to be, the bound alone decides.
No kernel may reach another device: no remote copies, remote signals or barrier semaphores. Data moves between devices by JAX's collectives and lax.ppermute only.
A program may use at most 128 MiB of HBM per device.

v0:
```python
import jax
import jax.numpy as jnp
from jax import lax
from jax.sharding import PartitionSpec as P

LAT = 48
LON = 128
ADVECTION_TOTAL = 4


def upstream_factors(rates, masks_now, advection_increment):
    east_rate = rates[advection_increment, 0].reshape(LAT, LON)
    north_rate = rates[advection_increment, 1].reshape(LAT, LON)
    east_mask = masks_now[advection_increment, 0].reshape(LAT, LON) == 1
    north_mask = masks_now[advection_increment, 1].reshape(LAT, LON) == 1
    remain = 1.0 - east_rate - north_rate
    from_west = jnp.where(east_mask, east_rate, 0.0)
    from_east = jnp.where(east_mask, 0.0, east_rate)
    from_south = jnp.where(north_mask, north_rate, 0.0)
    from_north = jnp.where(north_mask, 0.0, north_rate)
    return (remain, from_west, from_east, from_south, from_north)


def substep_move(values, weights):
    remain, from_west, from_east, from_south, from_north = weights
    west_cell = jnp.roll(values, 1, axis=2)
    east_cell = jnp.roll(values, -1, axis=2)
    zero_row = jnp.zeros_like(values[:, :1, :])
    south_cell = jnp.concatenate([zero_row, values[:, :-1, :]], axis=1)
    north_cell = jnp.concatenate([values[:, 1:, :], zero_row], axis=1)
    return (
        remain * values
        + from_west * west_cell
        + from_east * east_cell
        + from_south * south_cell
        + from_north * north_cell
    )


def apply_rows(rows_in, coefficient_series, cell_of_state, state_of_cell):
    count_rows = rows_in.shape[0]
    on_grid = jnp.take(rows_in, state_of_cell, axis=1).reshape(count_rows, LAT, LON)
    for weights in coefficient_series:
        on_grid = substep_move(on_grid, weights)
    return jnp.take(on_grid.reshape(count_rows, LAT * LON), cell_of_state, axis=1)


def shards(covariance, advective_ratio, flow_heading_flags, cell_of_state, added_uncertainty):
    local_rows = covariance.shape[0]
    total_states = LAT * LON
    devices = lax.axis_size(("row", "col"))
    first_row = lax.axis_index(("row", "col")) * local_rows
    state_of_cell = (
        jnp.zeros((total_states,), jnp.int32)
        .at[cell_of_state]
        .set(jnp.arange(total_states, dtype=jnp.int32))
    )
    column_index = lax.broadcasted_iota(jnp.int32, covariance.shape, 1)
    row_index = lax.broadcasted_iota(jnp.int32, covariance.shape, 0) + first_row
    on_diagonal = column_index == row_index
    spread_array = covariance
    rates = lax.all_gather(advective_ratio[0], ("row", "col"), axis=2, tiled=True)
    coefficient_series = [
        upstream_factors(rates, flow_heading_flags[0], advection_increment)
        for advection_increment in range(ADVECTION_TOTAL)
    ]
    one_side = apply_rows(spread_array, coefficient_series, cell_of_state, state_of_cell)
    blocks = one_side.reshape(local_rows, devices, local_rows)
    arrived = lax.all_to_all(blocks, ("row", "col"), split_axis=1, concat_axis=1, tiled=True)
    item_count = arrived.shape[2]
    turned = jnp.transpose(arrived, (2, 1, 0)).reshape(item_count, total_states)
    congruence_result = apply_rows(turned, coefficient_series, cell_of_state, state_of_cell)
    spread_array = congruence_result + jnp.where(on_diagonal, added_uncertainty[0][:, None], 0.0)
    return spread_array


def solution(mesh):
    in_specs = (
        P(("row", "col"), None),
        P(None, None, None, ("row", "col")),
        P(),
        P(),
        P(None, ("row", "col")),
    )
    out_specs = P(("row", "col"), None)
    return jax.shard_map(shards, mesh=mesh, in_specs=in_specs, out_specs=out_specs, check_vma=False)
```

profile of v0, /device:TPU:0, one launch (start us, length us, event | category | flops | bytes accessed | tf_op | source)
XLA Modules:
  0.0 1086.4 jit_solution(6866906980219342485)
XLA Ops:
  0.0 0.9 copy.14
  0.9 84.3 %all-gather = f32[1,4,2,6144]{1,2,0,3:T(2,128)} all-gather(f32[1,4,2,192]{1,2,0,3:T(2,128)S(1)} %copy.14), channel_id=2, replica_groups=mesh['row'=4,'col'=8] {'row','col'}, dimensions={3}, use_global_device_ids=true | all-gather | bytes 202752 | tf_op jit(solution)/shard_map/all_gather | solution.py:62
  85.2 5.8 copy.16
  91.0 267.0 %subtract_reduce_fusion.2 = (f32[6144]{0:T(1024)S(1)}, f32[6144]{0:T(1024)S(1)}, f32[6144]{0:T(1024)S(1)}, f32[6144]{0:T(1024)S(1)}, f32[6144]{0:T(1024)S(1)}, /...) fusion(f32[4,2,6144]{0,1,2:T(2,128)} %bitcast.38, ...), kind=kLoop, calls=%fused_computation.76 | loop fusion | flops 135168 | bytes 638976 | tf_op jit(solution)/shard_map/sub | solution.py:16
  358.1 199.8 %fusion.44 = (f32[6144]{0:T(1024)S(1)}, f32[6144]{0:T(1024)}, f32[6144]{0:T(1024)}, f32[6144]{0:T(1024)S(1)}, f32[6144]{0:T(1024)S(1)}, /*index=5*/f32[6144]{0:T...) fusion(s32[4,2,6144]{0,1,2:T(2,128)} %bitcast.41, f32[4,2,6144]{0,1,2:T(2,128)} %bitcast.39), kind=kLoop, calls=%fused_computation.90 | loop fusion | flops 104448 | bytes 614400 | tf_op jit(solution)/shard_map/jit(_where)/select_n | solution.py:17
  557.9 0.6 broadcast_clamp_fusion
  558.5 23.0 %scatter_custom_fusion = s32[6144]{0:T(1024)S(1)} fusion(s32[6144]{0:T(1024)S(1)} %get-tuple-element.84, s32[6144]{0:T(1024)S(1)} %iota.14, s32[]{:T(128)} %constant.4.clone.1), kind=kCustom, calls=%fused_computation.100 | custom fusion | bytes 24580 | tf_op jit(solution)/shard_map/scatter | solution.py:56
  581.5 6.4 copy.15
  588.0 26.5 %gather_fusion = f32[6144,192]{1,0:T(8,128)} fusion(f32[192,6144]{0,1:T(8,128)} %copy.15, s32[6144]{0:T(1024)S(1)} %fusion.48), kind=kCustom, calls=%fused_computation.clone | custom fusion | bytes 9461760 | tf_op jit(solution)/shard_map/jit(_take)/gather | solution.py:42
  614.5 5.3 broadcast_select_fusion.2
  619.8 6.4 fusion.73
  626.2 6.5 fusion.72
  632.6 0.1 fusion.74
  632.7 10.9 %fusion.3 = f32[192,48,128]{0,2,1:T(8,128)S(1)} fusion(f32[192,48,127]{0,2,1:T(8,128)} %get-tuple-element.80, f32[192,48,1]{0,2,1:T(1,128)S(1)} %get-tuple-element.82, f32[192,48,1]{0,2,1:T(1,128)S(1)} %get-tuple-element.81, f32[192,48,127]{0,2,1:T(8,128)} %get-tuple-element.79, f32[192,47,128]{0,2,1:T(8,128)} %get-tuple-element.78, ...), kind=kLoop, calls=%fused_computation.25 | loop fusion | flops 12976128 | bytes 28237824 | tf_op jit(solution)/shard_map/add | solution.py:32
  643.6 5.9 fusion.70
  649.6 6.5 fusion.69
  656.0 0.1 fusion.71
  656.1 11.6 %fusion.7 = f32[192,48,128]{0,2,1:T(8,128)} fusion(f32[192,48,127]{0,2,1:T(8,128)} %get-tuple-element.74, f32[192,48,1]{0,2,1:T(1,128)S(1)} %get-tuple-element.76, f32[192,48,1]{0,2,1:T(1,128)S(1)} %get-tuple-element.75, f32[192,48,127]{0,2,1:T(8,128)} %get-tuple-element.73, f32[192,47,128]{0,2,1:T(8,128)} %get-tuple-element.72, ...), kind=kLoop, calls=%fused_computation.31 | loop fusion | flops 12976128 | bytes 28237824 | tf_op jit(solution)/shard_map/add | solution.py:32
  667.7 11.5 %fusion.67 = (f32[192,48,127]{0,2,1:T(8,128)}, f32[192,48,127]{0,2,1:T(8,128)}) fusion(f32[192,48,128]{0,2,1:T(8,128)} %fusion.7), kind=kLoop, calls=%fused_computation.119 | loop fusion | bytes 18726912 | tf_op jit(solution)/shard_map/jit(_roll_static)/slice | solution.py:27
  679.2 6.5 fusion.66
  685.8 10.8 fusion.11
  696.6 5.9 fusion.64
  702.5 6.5 fusion.63
  709.0 0.8 compare_and_fusion
  709.8 11.9 %fusion.15 = f32[192,48,128]{0,2,1:T(8,128)} fusion(f32[192,48,127]{0,2,1:T(8,128)} %get-tuple-element.53, f32[192,48,1]{0,2,1:T(1,128)S(1)} %get-tuple-element.55, f32[192,48,1]{0,2,1:T(1,128)S(1)} %get-tuple-element.54, f32[192,48,127]{0,2,1:T(8,128)} %get-tuple-element.52, f32[192,47,128]{0,2,1:T(8,128)} %get-tuple-element.51, ...), kind=kLoop, calls=%fused_computation.43 | loop fusion | flops 12976128 | bytes 28237824 | tf_op jit(solution)/shard_map/add | solution.py:32
  721.7 28.5 %gather_fusion.1 = f32[6144,192]{1,0:T(8,128)} fusion(f32[192,6144]{0,1:T(8,128)} %bitcast.43, s32[6144]{0:T(1024)} %get-tuple-element.83), kind=kCustom, calls=%fused_computation.1.clone | custom fusion | bytes 9461760 | tf_op jit(solution)/shard_map/jit(_take)/gather | solution.py:45
  750.2 6.7 broadcast_select_fusion.1
  756.9 3.6 all-to-all-start
  760.5 0.6 iota_add_fusion
  761.1 139.3 %all-to-all-done = f32[192,32,192]{0,2,1:T(8,128)} async-done(((f32[192,32,192]{0,2,1:T(8,128)}), f32[192,32,192]{0,2,1:T(8,128)}, u32[]{:S(2)}, u32[]{:S(2)}) %all-to-all-start) | async-done | bytes 4718624 | tf_op jit(solution)/shard_map/all_to_all | solution.py:69
  900.4 6.9 copy.17
  907.3 26.5 %gather_fusion.2 = f32[6144,192]{1,0:T(8,128)} fusion(f32[192,6144]{0,1:T(8,128)} %bitcast.44, s32[6144]{0:T(1024)S(1)} %copy-done.6), kind=kCustom, calls=%fused_computation.2.clone | custom fusion | bytes 9461760 | tf_op jit(solution)/shard_map/jit(_take)/gather | solution.py:42
  933.8 5.3 broadcast_select_fusion
  939.1 6.4 fusion.61
  945.4 6.5 fusion.60
  952.0 10.9 %fusion.19 = f32[192,48,128]{0,2,1:T(8,128)S(1)} fusion(f32[192,48,127]{0,2,1:T(8,128)} %get-tuple-element.47, f32[192,48,1]{0,2,1:T(1,128)S(1)} %get-tuple-element.49, f32[192,48,1]{0,2,1:T(1,128)S(1)} %get-tuple-element.48, f32[192,48,127]{0,2,1:T(8,128)} %get-tuple-element.46, f32[192,47,128]{0,2,1:T(8,128)} %get-tuple-element.45, ...), kind=kLoop, calls=%fused_computation.49 | loop fusion | flops 12976128 | bytes 28237824 | tf_op jit(solution)/shard_map/add | solution.py:32
  962.9 5.9 fusion.58
  968.8 6.5 fusion.57
  975.4 11.6 %fusion.23 = f32[192,48,128]{0,2,1:T(8,128)} fusion(f32[192,48,127]{0,2,1:T(8,128)} %get-tuple-element.41, f32[192,48,1]{0,2,1:T(1,128)S(1)} %get-tuple-element.43, f32[192,48,1]{0,2,1:T(1,128)S(1)} %get-tuple-element.42, f32[192,48,127]{0,2,1:T(8,128)} %get-tuple-element.40, f32[192,47,128]{0,2,1:T(8,128)} %get-tuple-element.39, ...), kind=kLoop, calls=%fused_computation.55 | loop fusion | flops 12976128 | bytes 28237824 | tf_op jit(solution)/shard_map/add | solution.py:32
  987.0 11.5 %fusion.55 = (f32[192,48,127]{0,2,1:T(8,128)}, f32[192,48,127]{0,2,1:T(8,128)}) fusion(f32[192,48,128]{0,2,1:T(8,128)} %fusion.23), kind=kLoop, calls=%fused_computation.107 | loop fusion | bytes 18726912 | tf_op jit(solution)/shard_map/jit(_roll_static)/slice | solution.py:27
  998.5 6.5 fusion.54
  1005.0 11.6 %fusion.27 = f32[192,48,128]{0,2,1:T(8,128)} fusion(f32[192,48,127]{0,2,1:T(8,128)} %get-tuple-element.35, f32[192,48,1]{0,2,1:T(1,128)S(1)} %get-tuple-element.37, f32[192,48,1]{0,2,1:T(1,128)S(1)} %get-tuple-element.36, f32[192,48,127]{0,2,1:T(8,128)} %get-tuple-element.34, f32[192,47,128]{0,2,1:T(8,128)} %get-tuple-element.33, ...), kind=kLoop, calls=%fused_computation.61 | loop fusion | flops 12976128 | bytes 28237824 | tf_op jit(solution)/shard_map/add | solution.py:32
  1016.6 11.5 %fusion.52 = (f32[192,48,127]{0,2,1:T(8,128)}, f32[192,48,127]{0,2,1:T(8,128)}) fusion(f32[192,48,128]{0,2,1:T(8,128)} %fusion.27), kind=kLoop, calls=%fused_computation.104 | loop fusion | bytes 18726912 | tf_op jit(solution)/shard_map/jit(_roll_static)/slice | solution.py:27
  1028.1 6.5 fusion.51
  1034.7 11.6 %fusion.31 = f32[192,48,128]{0,2,1:T(8,128)} fusion(f32[192,48,127]{0,2,1:T(8,128)} %get-tuple-element.29, f32[192,48,1]{0,2,1:T(1,128)S(1)} %get-tuple-element.31, f32[192,48,1]{0,2,1:T(1,128)S(1)} %get-tuple-element.30, f32[192,48,127]{0,2,1:T(8,128)} %get-tuple-element.28, f32[192,47,128]{0,2,1:T(8,128)} %get-tuple-element.27, ...), kind=kLoop, calls=%fused_computation.67 | loop fusion | flops 12976128 | bytes 28237824 | tf_op jit(solution)/shard_map/add | solution.py:32
  1046.3 26.5 %gather_fusion.3 = f32[6144,192]{1,0:T(8,128)} fusion(f32[192,6144]{0,1:T(8,128)} %bitcast.42, s32[6144]{0:T(1024)S(1)} %copy-done.7), kind=kCustom, calls=%fused_computation.3.clone | custom fusion | bytes 9461760 | tf_op jit(solution)/shard_map/jit(_take)/gather | solution.py:45
  1072.9 7.0 bitcast_add_fusion
  1079.8 6.1 copy.18
  (33 shorter events, 0.5 us)
Async XLA Ops:
  0.0 85.2 %copy-start.8 = (s32[1,4,2,6144]{3,2,1,0:T(2,128)S(1)}, s32[1,4,2,6144]{3,2,1,0:T(2,128)}, u32[]{:S(2)}) copy-start(s32[1,4,2,6144]{3,2,1,0:T(2,128)} %param.9) | copy-start | bytes 589828
  358.1 199.8 %copy-start.9 = (s32[6144]{0:T(1024)S(1)}, s32[6144]{0:T(1024)}, u32[]{:S(2)}) copy-start(s32[6144]{0:T(1024)} %param.10) | copy-start | bytes 73732
  581.5 6.5 copy-start.5
  619.8 12.9 %copy-start.4 = (f32[6144,192]{1,0:T(8,128)}, f32[6144,192]{1,0:T(8,128)S(1)}, u32[]{:S(2)}) copy-start(f32[6144,192]{1,0:T(8,128)S(1)} %broadcast_select_fusion.2) | copy-start | bytes 14155780
  667.7 11.5 %copy-start.2 = (f32[192,48,128]{0,2,1:T(8,128)S(1)}, f32[192,48,128]{0,2,1:T(8,128)}, u32[]{:S(2)}) copy-start(f32[192,48,128]{0,2,1:T(8,128)} %fusion.7) | copy-start | bytes 14155780
  756.9 143.5 %all-to-all-start = ((f32[192,32,192]{0,2,1:T(8,128)}), f32[192,32,192]{0,2,1:T(8,128)}, u32[]{:S(2)}, u32[]{:S(2)}) async-start(f32[192,32,192]{0,2,1:T(8,128)} %bitcast.53), calls=%async_computation | async-start | bytes 12582912 | tf_op jit(solution)/shard_map/all_to_all | solution.py:69
  900.4 6.9 copy-start.6
  939.1 12.9 %copy-start.3 = (f32[6144,192]{1,0:T(8,128)}, f32[6144,192]{1,0:T(8,128)S(1)}, u32[]{:S(2)}) copy-start(f32[6144,192]{1,0:T(8,128)S(1)} %broadcast_select_fusion) | copy-start | bytes 14155780
  987.0 11.5 %copy-start = (f32[192,48,128]{0,2,1:T(8,128)S(1)}, f32[192,48,128]{0,2,1:T(8,128)}, u32[]{:S(2)}) copy-start(f32[192,48,128]{0,2,1:T(8,128)} %fusion.23) | copy-start | bytes 14155780
  1016.6 11.5 %copy-start.1 = (f32[192,48,128]{0,2,1:T(8,128)S(1)}, f32[192,48,128]{0,2,1:T(8,128)}, u32[]{:S(2)}) copy-start(f32[192,48,128]{0,2,1:T(8,128)} %fusion.27) | copy-start | bytes 14155780
  1034.7 11.6 %copy-start.7 = (s32[6144]{0:T(1024)S(1)}, s32[6144]{0:T(1024)}, u32[]{:S(2)}) copy-start(s32[6144]{0:T(1024)} %get-tuple-element.83) | copy-start | bytes 73732
  1046.3 26.5 %copy-start.10 = (f32[1,192]{1,0:T(1,128)S(1)}, f32[1,192]{1,0:T(1,128)}, u32[]{:S(2)}) copy-start(f32[1,192]{1,0:T(1,128)} %param.11) | copy-start | bytes 2308
  1046.3 26.5 %copy-start.11 = (s32[192]{0:T(256)S(1)}, s32[192]{0:T(256)}, u32[]{:S(2)}) copy-start(s32[192]{0:T(256)} %iota_add_fusion) | copy-start | bytes 2308
where the time goes:
time: 1090 us
  other arithmetic  584 us (54%)
  local copies, waits for them, and re-layouts  275 us (25%)
  waiting for transfers between devices  139 us (13%)
  blocking collectives  84.3 us (8%)
    sub x1, other arithmetic, upstream_factors(): remain = 1.0 - east_rate - north_rate  267 us
    select_n x1, other arithmetic, upstream_factors(): from_west = jnp.where(east_mask, east_rate, 0.0)  200 us
    all_to_all x1, waiting for transfers between devices, shards(): lax.all_to_all(blocks, ('row', 'col'), split_axis=1, concat_axis=1, tiled...  139 us
    add x8, other arithmetic, substep_move(): remain * values + from_west * west_cell + from_east * east_cell  90.9 us
    all_gather x1, blocking collectives, shards(): lax.all_gather(advective_ratio[0], ('row', 'col'), axis=2, tiled=True)  84.3 us
    slice x16, local copies, waits for them, and re-layouts, substep_move(): east_cell = jnp.roll(values, -1, axis=2)  65.5 us
    gather x2, local copies, waits for them, and re-layouts, apply_rows(): jnp.take(on_grid.reshape(count_rows, LAT * LON), cell_of_state, axis=1)  55 us
    gather x2, local copies, waits for them, and re-layouts, apply_rows(): jnp.take(rows_in, state_of_cell, axis=1).reshape(count_rows, LAT, LON)  53 us
  transfers between devices with their start and end apart: 1, of which 1 were waited for; matrix products, arithmetic and copies ran while one was open for 0% of the time, Pallas kernels for 0%

commit v1 on v0

v1 whole, which is shorter than its diff:
```python
import jax
import jax.numpy as jnp
from jax import lax
from jax.experimental import pallas as pl
from jax.experimental.pallas import tpu as pltpu
from jax.sharding import PartitionSpec as P

LAT = 48
LON = 128
ADVECTION_TOTAL = 4
CELLS = LAT * LON
LANES = 128
AXES = ("row", "col")
GROUPS = 8
UNROLL = 32


def spans_first(count):
    half = count // 2
    return ((0, half), (half, half))


def spans_second(count):
    return tuple((at, min(LANES, count - at)) for at in range(0, count, LANES))


def block_rows(count):
    full, rest = divmod(count, LANES)
    if rest * 2 == LANES:
        return full * count + count // 2
    return (full + (rest > 0)) * count


def scatter_rows(index, source, target, start, stop):
    def body(step, carry):
        base = step * UNROLL
        rows = [source[pl.ds(pl.multiple_of(2 * (base + u), 2), 2), :] for u in range(UNROLL)]
        for u in range(UNROLL):
            target[pl.ds(pl.multiple_of(index[base + u], 2), 2), :] = rows[u]
        return carry

    lax.fori_loop(start // UNROLL, stop // UNROLL, body, 0)


def gather_rows(index, source, target, start, stop):
    def body(step, carry):
        base = step * UNROLL
        rows = [source[pl.ds(pl.multiple_of(index[base + u], 2), 2), :] for u in range(UNROLL)]
        for u in range(UNROLL):
            target[pl.ds(pl.multiple_of(2 * (base + u), 2), 2), :] = rows[u]
        return carry

    lax.fori_loop(start // UNROLL, stop // UNROLL, body, 0)


def advect(spans, coefs, picks, packed, spare, level_a, level_b):
    count = level_a.shape[1]

    def to_grid(i, carry):
        for h, (at, width) in enumerate(spans):
            block = packed[pl.ds(2 * LON * i + h, LON, stride=2), :]
            level_a[i + 1, at : at + width, :] = block.T[:width]
        return carry

    lax.fori_loop(0, LAT, to_grid, 0)
    for level in (level_a, level_b):
        for edge in (0, LAT + 1):
            level[edge] = jnp.zeros((count, LON), jnp.float32)

    for s in range(ADVECTION_TOTAL):
        source, target = (level_a, level_b) if s % 2 == 0 else (level_b, level_a)

        def row(i, carry, s=s, source=source, target=target):
            def spread(ref, which):
                return jnp.broadcast_to(ref[s, which, pl.ds(i, 1), :], (8, LON))

            remain, rate_x, rate_y = (spread(coefs, w) for w in range(3))
            pick_x, north = (spread(picks, w) for w in range(2))
            from_south = north == 1
            for g in range(0, count, 8):
                here = source[i + 1, g : g + 8, :]
                side = jnp.take_along_axis(here, pick_x, axis=1)
                below = source[i, g : g + 8, :]
                above = source[i + 2, g : g + 8, :]
                target[i + 1, g : g + 8, :] = (
                    remain * here + rate_x * side + rate_y * jnp.where(from_south, below, above)
                )
            return carry

        lax.fori_loop(0, LAT, row, 0)
    final = level_a if ADVECTION_TOTAL % 2 == 0 else level_b

    def to_cells(i, carry):
        for h, (at, width) in enumerate(spans):
            spare[pl.ds(2 * LON * i + h, LON, stride=2), 0:width] = final[i + 1, at : at + width, :].T
        return carry

    lax.fori_loop(0, LAT, to_cells, 0)


def first_pass(index, x_hbm, coefs, picks, o_hbm, x_v, k_a, k_b, level_a, level_b, o_v, sem_in, sem_out):
    count = x_v.shape[0]
    devices = o_v.shape[0]
    spans = spans_first(count)
    wide = CELLS // GROUPS

    def fetch(q):
        part = pl.ds(q * wide, wide)
        return pltpu.make_async_copy(x_hbm.at[:, part], x_v.at[:, part], sem_in.at[q])

    for q in range(GROUPS):
        fetch(q).start()

    def turn(c, carry):
        at_lane = pl.multiple_of(c * LANES, LANES)
        for h, (at, width) in enumerate(spans):
            k_a[pl.ds(2 * LANES * c + h, LANES, stride=2), 0:width] = x_v[at : at + width, pl.ds(at_lane, LANES)].T
        return carry

    each = wide // LANES
    for q in range(GROUPS):
        fetch(q).wait()
        lax.fori_loop(q * each, (q + 1) * each, turn, 0)
    scatter_rows(index, k_a, k_b, 0, CELLS)
    advect(spans, coefs, picks, k_b, k_a, level_a, level_b)
    gather_rows(index, k_a, k_b, 0, CELLS)
    full, rest = divmod(count, LANES)

    def pack(e, carry):
        base = 2 * count * e
        for t, (at_m, width_m) in enumerate(spans_second(count)):
            rows = [k_b[pl.ds(base + 2 * at_m + h, width_m, stride=2), :] for h in range(2)]
            half = count // 2
            if t == full and 2 * rest == LANES:
                o_v[e, full * count : full * count + half, :] = jnp.concatenate(rows, axis=0).T[:half]
            else:
                for h in range(2):
                    o_v[e, t * count + h * half : t * count + (h + 1) * half, 0:width_m] = rows[h].T[:half]
        return carry

    some = devices // GROUPS

    def send(q):
        part = pl.ds(q * some, some)
        return pltpu.make_async_copy(o_v.at[part], o_hbm.at[part], sem_out.at[q])

    for q in range(GROUPS):
        lax.fori_loop(q * some, (q + 1) * some, pack, 0)
        send(q).start()
    for q in range(GROUPS):
        send(q).wait()


def second_pass(index, place, a_hbm, coefs, picks, extra, o_hbm, a_v, k_a, k_b, level_a, level_b, o_v, sem_in, sem_out):
    count = o_v.shape[0]
    devices = a_v.shape[0]
    spans = spans_second(count)
    full, rest = divmod(count, LANES)
    half = count // 2
    some = devices // GROUPS

    def fetch(q):
        part = pl.ds(q * some, some)
        return pltpu.make_async_copy(a_hbm.at[part], a_v.at[part], sem_in.at[q])

    for q in range(GROUPS):
        fetch(q).start()

    def unpack(d, carry):
        base = 2 * count * d
        for t in range(len(spans)):
            if t == full and 2 * rest == LANES:
                both = a_v[d, full * count : full * count + half, :]
                k_a[pl.ds(base + t, half, stride=2), :] = both
                k_a[pl.ds(base + 2 * half + t, half, stride=2), :] = pltpu.roll(both, LANES // 2, 1)
            else:
                k_a[pl.ds(base + t, count, stride=2), :] = a_v[d, t * count : (t + 1) * count, :]
        return carry

    for q in range(GROUPS):
        fetch(q).wait()
        lax.fori_loop(q * some, (q + 1) * some, unpack, 0)
    scatter_rows(index, k_a, k_b, 0, CELLS)
    advect(spans, coefs, picks, k_b, k_a, level_a, level_b)
    gather_rows(index, k_a, k_b, 0, CELLS)
    mine = pl.ds(pl.multiple_of(2 * count * place[0], 16), 2 * count)
    k_b[mine, :] = k_b[mine, :] + extra[...]

    def turn(c, carry):
        at_lane = pl.multiple_of(c * LANES, LANES)
        for h, (at, width) in enumerate(spans):
            o_v[at : at + width, pl.ds(at_lane, LANES)] = k_b[pl.ds(2 * LANES * c + h, LANES, stride=2), :].T[:width]
        return carry

    wide = CELLS // GROUPS
    each = wide // LANES

    def send(q):
        part = pl.ds(q * wide, wide)
        return pltpu.make_async_copy(o_v.at[:, part], o_hbm.at[:, part], sem_out.at[q])

    for q in range(GROUPS):
        lax.fori_loop(q * each, (q + 1) * each, turn, 0)
        send(q).start()
    for q in range(GROUPS):
        send(q).wait()


def scratch(first, count, last):
    return [
        pltpu.VMEM(first, jnp.float32),
        pltpu.VMEM((2 * CELLS, LANES), jnp.float32),
        pltpu.VMEM((2 * CELLS, LANES), jnp.float32),
        pltpu.VMEM((LAT + 2, count, LON), jnp.float32),
        pltpu.VMEM((LAT + 2, count, LON), jnp.float32),
        pltpu.VMEM(last, jnp.float32),
        pltpu.SemaphoreType.DMA((GROUPS,)),
        pltpu.SemaphoreType.DMA((GROUPS,)),
    ]


def shards(covariance, advective_ratio, flow_heading_flags, cell_of_state, added_uncertainty):
    count = covariance.shape[0]
    devices = lax.axis_size(AXES)
    here = lax.axis_index(AXES)
    rows = block_rows(count)
    smem = pl.BlockSpec(memory_space=pltpu.SMEM)
    vmem = pl.BlockSpec(memory_space=pltpu.VMEM)
    hbm = pl.BlockSpec(memory_space=pl.ANY)
    params = pltpu.CompilerParams(vmem_limit_bytes=60 * 2**20)

    own = advective_ratio[0].reshape(1, ADVECTION_TOTAL * 2, count)
    spread = jnp.broadcast_to(own, (devices, ADVECTION_TOTAL * 2, count))
    rates = lax.all_to_all(spread, AXES, split_axis=0, concat_axis=0, tiled=True)
    rates = jnp.transpose(rates, (1, 0, 2)).reshape(ADVECTION_TOTAL, 2, LAT, LON)
    heading = flow_heading_flags[0].reshape(ADVECTION_TOTAL, 2, LAT, LON)
    rate_x, rate_y = rates[:, 0], rates[:, 1]
    coefs = jnp.stack([1.0 - rate_x - rate_y, rate_x, rate_y], axis=1)
    lane = lax.broadcasted_iota(jnp.int32, (ADVECTION_TOTAL, LAT, LON), 2)
    pick_x = jnp.where(heading[:, 0] == 1, lane + (LON - 1), lane + 1) % LON
    picks = jnp.stack([pick_x, heading[:, 1]], axis=1)
    index = 2 * cell_of_state

    blocks = pl.pallas_call(
        first_pass,
        out_shape=jax.ShapeDtypeStruct((devices, rows, LANES), jnp.float32),
        in_specs=[smem, hbm, vmem, vmem],
        out_specs=hbm,
        scratch_shapes=scratch((count, CELLS), count, (devices, rows, LANES)),
        compiler_params=params,
        name="first_pass",
    )(index, covariance, coefs, picks)
    arrived = lax.all_to_all(blocks, AXES, split_axis=0, concat_axis=0, tiled=True)

    state = lax.broadcasted_iota(jnp.int32, (count, 2, LANES), 0)
    slot = lax.broadcasted_iota(jnp.int32, (count, 2, LANES), 1) * LANES
    slot = slot + lax.broadcasted_iota(jnp.int32, (count, 2, LANES), 2)
    extra = jnp.where(state == slot, added_uncertainty[0][:, None, None], 0.0).reshape(2 * count, LANES)
    return pl.pallas_call(
        second_pass,
        out_shape=jax.ShapeDtypeStruct((count, CELLS), jnp.float32),
        in_specs=[smem, smem, hbm, vmem, vmem, vmem],
        out_specs=hbm,
        scratch_shapes=scratch((devices, rows, LANES), count, (count, CELLS)),
        compiler_params=params,
        name="second_pass",
    )(index, here.reshape(1), arrived, coefs, picks, extra)


def solution(mesh):
    in_specs = (
        P(AXES, None),
        P(None, None, None, AXES),
        P(),
        P(),
        P(None, AXES),
    )
    return jax.shard_map(shards, mesh=mesh, in_specs=in_specs, out_specs=P(AXES, None), check_vma=False)
```

time: 1090 us -> 233 us (0.21)
  other arithmetic: 584 us -> 3.78 us
  local copies, waits for them, and re-layouts: 275 us -> 3.27 us
  Pallas kernels: 0 us -> 103 us
  blocking collectives: 84.3 us -> 0 us
  waiting for transfers between devices: 139 us -> 112 us
    sub x1, other arithmetic: 267 us -> 0.01 us  [shards(): coefs = jnp.stack([1.0 - rate_x - rate_y, rate_x, rate_y], axis=1)]
    select_n x4 -> x2, other arithmetic: 217 us -> 0.96 us  [the longest x1 0.91 us: shards(): jnp.where(state == slot, added_uncertainty[0][:, None, None], 0.0)]
    slice x24 -> x0, local copies, waits for them, and re-layouts: 117 us -> none  [the longest x16 65.5 us: substep_move(): east_cell = jnp.roll(values, -1, axis=2)]
    gather x4 -> x0, local copies, waits for them, and re-layouts: 108 us -> none  [the longest x2 55 us: apply_rows(): jnp.take(on_grid.reshape(count_rows, LAT * LON), cell_of_state, axis=1)]
    pallas_call x0 -> x2, Pallas kernels: none -> 103 us  [the longest x1 51.8 us: shards(): pl.pallas_call(first_pass, out_shape=jax.ShapeDtypeStruct((devices, rows,...]
    add x10 -> x1, other arithmetic: 98.5 us -> 0.01 us  [shards(): pick_x = jnp.where(heading[:, 0] == 1, lane + (LON - 1), lane + 1) % LON]
    all_gather x1 -> x0, blocking collectives: 84.3 us -> none  [shards(): lax.all_gather(advective_ratio[0], ('row', 'col'), axis=2, tiled=True)]
    all_to_all x1 -> x2, waiting for transfers between devices: 139 us -> 112 us  [the longest x1 105 us: shards(): lax.all_to_all(blocks, AXES, split_axis=0, concat_axis=0, tiled=True)]
  transfers between devices with their start and end apart: 1 -> 2, of which waited for: 1 -> 2; matrix products, arithmetic and copies ran while one was open for 0% -> 2% of each run, Pallas kernels for 0% -> 0%
where the time goes in v1:
time: 233 us; the launch traced here: 232 us
  waiting for transfers between devices  112 us (48%)
  Pallas kernels  103 us (44%)
  starting transfers between devices  10.9 us (5%)
  other arithmetic  3.78 us (2%)
  local copies, waits for them, and re-layouts  3.27 us (1%)
    all_to_all x1, waiting for transfers between devices, shards(): lax.all_to_all(blocks, AXES, split_axis=0, concat_axis=0, tiled=True)  105 us
    pallas_call x1, Pallas kernels, shards(): pl.pallas_call(first_pass, out_shape=jax.ShapeDtypeStruct((devices, rows,...  51.8 us
    pallas_call x1, Pallas kernels, shards(): pl.pallas_call(second_pass, out_shape=jax.ShapeDtypeStruct((count, CELLS)...  51 us
    all_to_all x1, starting transfers between devices, shards(): lax.all_to_all(spread, AXES, split_axis=0, concat_axis=0, tiled=True)  7.33 us
    all_to_all x1, waiting for transfers between devices, shards(): lax.all_to_all(spread, AXES, split_axis=0, concat_axis=0, tiled=True)  6.79 us
  transfers between devices with their start and end apart: 2, of which 2 were waited for; matrix products, arithmetic and copies ran while one was open for 2% of the time, Pallas kernels for 0%

profile of v1, /device:TPU:0, one launch (start us, length us, event | category | flops | bytes accessed | tf_op | source)
XLA Modules:
  0.0 232.4 jit_solution(13517164701175610029)
XLA Ops:
  0.0 0.7 broadcast_in_dim.25
  0.7 0.7 broadcast_in_dim.26
  1.4 7.3 %all-to-all-start = ((f32[32,8,192]{2,1,0:T(8,128)}), f32[32,8,192]{2,1,0:T(8,128)S(1)}, u32[]{:S(2)}, u32[]{:S(2)}) async-start(f32[32,8,192]{2,1,0:T(8,128)} %broadcast_in_dim.26), calls=%async_computation | async-start | bytes 524288 | tf_op jit(solution)/shard_map/all_to_all | solution.py:234
  8.8 1.1 reshape_squeeze.4
  9.9 0.7 pad_add_fusion.picks
  10.6 1.3 broadcast_multiply_fusion.index
  12.0 6.8 %all-to-all-done = f32[32,8,192]{2,1,0:T(8,128)S(1)} async-done(((f32[32,8,192]{2,1,0:T(8,128)}), f32[32,8,192]{2,1,0:T(8,128)S(1)}, u32[]{:S(2)}, u32[]{:S(2)}) %all-to-all-start) | async-done | bytes 196640 | tf_op jit(solution)/shard_map/all_to_all | solution.py:234
  18.8 0.1 copy.6
  18.9 0.1 reshape.14
  19.0 0.8 pad_maximum_fusion.coefs
  19.8 51.8 %first_pass.1 = f32[32,288,128]{2,1,0:T(8,128)} custom-call(s32[6144]{0:T(1024)} %broadcast_multiply_fusion.index, f32[192,6144]{1,0:T(8,128)} %x_hbm.1, f32[4,3,48,128]{3,2,1,0:T(8,128)} %pad_maximum_fusion.coefs, s32[4,2,48,128]{3,2,1,0:T(8,128)} %pad_add_fusion.picks), custom_call_target="tpu_custom_call" | custom-call | tf_op jit(solution)/shard_map/first_pass/pallas_call | solution.py:244
  71.6 0.0 copy-start
  71.6 3.6 %all-to-all-start.1 = ((f32[32,288,128]{2,1,0:T(8,128)}), f32[32,288,128]{2,1,0:T(8,128)}, u32[]{:S(2)}, u32[]{:S(2)}) async-start(f32[32,288,128]{2,1,0:T(8,128)} %first_pass.1), calls=%async_computation.1 | async-start | bytes 9437184 | tf_op jit(solution)/shard_map/all_to_all | solution.py:253
  75.2 0.1 iota.46
  75.3 0.0 copy-done
  75.4 0.1 broadcast_in_dim.28
  75.4 0.1 broadcast_in_dim.29
  75.6 0.1 iota.42
  75.8 0.9 fusion.extra
  76.7 104.7 %all-to-all-done.1.a_hbm = f32[32,288,128]{2,1,0:T(8,128)} async-done(((f32[32,288,128]{2,1,0:T(8,128)}), f32[32,288,128]{2,1,0:T(8,128)}, u32[]{:S(2)}, u32[]{:S(2)}) %all-to-all-start.1) | async-done | bytes 4718624 | tf_op jit(solution)/shard_map/all_to_all | solution.py:253
  181.4 51.0 %second_pass.1 = f32[192,6144]{1,0:T(8,128)} custom-call(s32[6144]{0:T(1024)} %broadcast_multiply_fusion.index, s32[1]{0:T(128)} %bitcast.place, f32[32,288,128]{2,1,0:T(8,128)} %all-to-all-done.1.a_hbm, f32[4,3,48,128]{3,2,1,0:T(8,128)} %pad_maximum_fusion.coefs, s32[4,2,48,128]{3,2,1,0:T(8,128)} %pad_add_fusion.picks, f32[384,128]{1,0:T(8,128)} %fusion.extra), custom_call_target="tpu_custom_call" | custom-call | tf_op jit(solution)/shard_map/second_pass/pallas_call | solution.py:259
  (6 shorter events, 0.1 us)
Async XLA Ops:
  1.4 17.3 %all-to-all-start = ((f32[32,8,192]{2,1,0:T(8,128)}), f32[32,8,192]{2,1,0:T(8,128)S(1)}, u32[]{:S(2)}, u32[]{:S(2)}) async-start(f32[32,8,192]{2,1,0:T(8,128)} %broadcast_in_dim.26), calls=%async_computation | async-start | bytes 524288 | tf_op jit(solution)/shard_map/all_to_all | solution.py:234
  71.6 3.8 %copy-start = (f32[1,192]{1,0:T(1,128)S(1)}, f32[1,192]{1,0:T(1,128)}, u32[]{:S(2)}) copy-start(f32[1,192]{1,0:T(1,128)} %param.9) | copy-start | bytes 2308
  71.6 109.8 %all-to-all-start.1 = ((f32[32,288,128]{2,1,0:T(8,128)}), f32[32,288,128]{2,1,0:T(8,128)}, u32[]{:S(2)}, u32[]{:S(2)}) async-start(f32[32,288,128]{2,1,0:T(8,128)} %first_pass.1), calls=%async_computation.1 | async-start | bytes 9437184 | tf_op jit(solution)/shard_map/all_to_all | solution.py:253

commit v2 on v0

v2 whole, which is shorter than its diff:
```python
import jax
import jax.numpy as jnp
from jax import lax
from jax.experimental import pallas as pl
from jax.experimental.pallas import tpu as pltpu
from jax.sharding import PartitionSpec as P

LAT = 48
LON = 128
ADVECTION_TOTAL = 4
CELLS = LAT * LON
LANES = 128
AXES = ("row", "col")
GROUPS = 8
BATCH = 16
LAG = 2
RING = 8
MIB = 2**20


def spans_first(count):
    half = count // 2
    return ((0, half), (half, half))


def spans_second(count):
    return tuple((at, min(LANES, count - at)) for at in range(0, count, LANES))


def is_packed(count, width):
    return 2 * width == LANES and count > width


def scatter_rows(index, start, source, first, target, slots, total):
    for u0 in range(0, total, BATCH):
        some = range(u0, min(u0 + BATCH, total))
        rows = [source[pl.ds(first + slots * u, slots), :] for u in some]
        for u, row in zip(some, rows):
            target[pl.ds(pl.multiple_of(slots * index[start + u], slots), slots), :] = row


def gather_rows(index, start, source, target, slots, total):
    for u0 in range(0, total, BATCH):
        some = range(u0, min(u0 + BATCH, total))
        rows = [source[pl.ds(pl.multiple_of(slots * index[start + u], slots), slots), :] for u in some]
        for u, row in zip(some, rows):
            target[slots * u : slots * (u + 1), :] = row


def slot_rows(start, h, total, slots):
    return pl.ds(start + h, total, stride=slots) if slots > 1 else pl.ds(start, total)


def substep(coefs, picks, s, source, target, i):
    def spread(ref, which):
        return jnp.broadcast_to(ref[s, which, pl.ds(i, 1), :], (8, LON))

    remain, rate_x, rate_y = (spread(coefs, w) for w in range(3))
    pick_x, north = (spread(picks, w) for w in range(2))
    from_south = north == 1
    south, middle, above = ((i + d) & (RING - 1) for d in (-1, 0, 1))
    for g in range(0, source.shape[1], 8):
        here = source[middle, g : g + 8, :]
        side = jnp.take_along_axis(here, pick_x, axis=1)
        y_side = jnp.where(from_south, source[south, g : g + 8, :], source[above, g : g + 8, :])
        target[middle, g : g + 8, :] = remain * here + rate_x * side + rate_y * y_side


def advect(spans, coefs, picks, cells_in, cells_out, levels):
    slots = len(spans)
    count = levels[0].shape[1]

    def enter(i):
        for h, (at, width) in enumerate(spans):
            block = cells_in[slot_rows(slots * LON * i, h, LON, slots), :]
            levels[0][i & (RING - 1), at : at + width, :] = block.T[:width]

    def leave(i):
        for h, (at, width) in enumerate(spans):
            block = levels[-1][i & (RING - 1), at : at + width, :]
            cells_out[slot_rows(slots * LON * i, h, LON, slots), 0:width] = block.T

    for level in levels[:-1]:
        level[RING - 1] = jnp.zeros((count, LON), jnp.float32)
    tail = LAG * ADVECTION_TOTAL + 1

    def step(i, guard):
        def run(stage, j):
            if guard:
                pl.when((j >= 0) & (j < LAT))(lambda: stage(j))
            else:
                stage(j)

        run(leave, i - tail)
        for s in reversed(range(ADVECTION_TOTAL)):
            run(lambda j, s=s: substep(coefs, picks, s, levels[s], levels[s + 1], j), i - LAG * (s + 1))
        run(enter, i)

    def guarded(i, carry):
        step(i, True)
        return carry

    def steady(i, carry):
        step(i, False)
        return carry

    lax.fori_loop(0, tail, guarded, 0)
    lax.fori_loop(tail, LAT, steady, 0)
    lax.fori_loop(LAT, LAT + tail, guarded, 0)


def lay_on_grid(index, x_hbm, o_ref, x_v, tiles, sem_in):
    spans = spans_first(x_v.shape[0])
    slots = len(spans)
    wide = CELLS // GROUPS
    each = wide // LANES

    def fetch(q):
        part = pl.ds(q * wide, wide)
        return pltpu.make_async_copy(x_hbm.at[:, part], x_v.at[:, part], sem_in.at[q])

    for q in range(GROUPS):
        fetch(q).start()

    def turn(c, slot):
        at_lane = pl.multiple_of(c * LANES, LANES)
        for h, (at, width) in enumerate(spans):
            block = x_v[at : at + width, pl.ds(at_lane, LANES)]
            tiles[slot][slot_rows(0, h, LANES, slots), 0:width] = block.T

    def place(c, slot):
        scatter_rows(index, c * LANES, tiles[slot], 0, o_ref, slots, LANES)

    fetch(0).wait()
    turn(0, 0)

    def body(b, carry):
        c = 2 * b
        turn(c + 1, 1)
        place(c, 0)
        turn(jnp.minimum(c + 2, CELLS // LANES - 1), 0)
        place(c + 1, 1)
        return carry

    for q in range(GROUPS):
        if q + 1 < GROUPS:
            fetch(q + 1).wait()
        lax.fori_loop(q * each // 2, (q + 1) * each // 2, body, 0)


def send_part(index, cells, o_v, o_hbm, tiles, sem_out, count, at, width):
    spans = spans_first(count)
    slots = len(spans)
    half = count // 2
    devices = o_v.shape[0]
    some = devices // GROUPS

    def pick(e, slot):
        gather_rows(index, e * count + at, cells, tiles[slot], slots, width)

    def turn(e, slot):
        rows = [tiles[slot][slot_rows(0, h, width, slots), :] for h in range(slots)]
        if is_packed(count, width):
            o_v[e] = jnp.concatenate(rows, axis=0).T[:half]
        else:
            for h in range(slots):
                o_v[e, h * half : (h + 1) * half, 0:width] = rows[h].T[:half]

    def send(q):
        part = pl.ds(q * some, some)
        return pltpu.make_async_copy(o_v.at[part], o_hbm.at[part], sem_out.at[q])

    pick(0, 0)

    def body(b, carry):
        e = 2 * b
        pick(e + 1, 1)
        turn(e, 0)
        pick(jnp.minimum(e + 2, devices - 1), 0)
        turn(e + 1, 1)
        return carry

    for q in range(GROUPS):
        lax.fori_loop(q * some // 2, (q + 1) * some // 2, body, 0)
        send(q).start()
    for q in range(GROUPS):
        send(q).wait()


def first_pass(count, at, width):
    def kernel(index, x_hbm, coefs, picks, o_hbm, keep_hbm, x_v, cells_in, cells_out, o_v, tile_a, tile_b, sem_in, sem_out, sem_keep, *levels):
        tiles = (tile_a, tile_b)
        lay_on_grid(index, x_hbm, cells_in, x_v, tiles, sem_in)
        advect(spans_first(count), coefs, picks, cells_in, cells_out, levels)
        keep = pltpu.make_async_copy(cells_out, keep_hbm, sem_keep)
        keep.start()
        send_part(index, cells_out, o_v, o_hbm, tiles, sem_out, count, at, width)
        keep.wait()

    return kernel


def first_rest(count, at, width):
    def kernel(index, cells, o_hbm, o_v, tile_a, tile_b, sem_out):
        send_part(index, cells, o_v, o_hbm, (tile_a, tile_b), sem_out, count, at, width)

    return kernel


def second_pass(count, devices, at, width):
    packed = is_packed(count, width)
    rows = count // 2 if packed else count

    def kernel(index, place, a_hbm, coefs, picks, extra, *rest):
        if at:
            rest = rest[1:]
        o_hbm, a_v, cells_in, cells_out, o_v, tile_a, tile_b, sem_in, sem_out, *levels = rest
        tiles = (tile_a, tile_b)
        some = devices // GROUPS

        def fetch(q):
            part = pl.ds(q * some * rows, some * rows)
            return pltpu.make_async_copy(a_hbm.at[part], a_v.at[part], sem_in.at[q])

        for q in range(GROUPS):
            fetch(q).start()

        def arrive(d, carry):
            at_row = pl.multiple_of(d * rows, 8)
            if packed:
                tile_a[0:rows, :] = pltpu.roll(a_v[pl.ds(at_row, rows), :], LANES // 2, 1)
                scatter_rows(index, d * count, a_v, at_row, cells_in, 1, rows)
                scatter_rows(index, d * count + rows, tile_a, 0, cells_in, 1, rows)
            else:
                scatter_rows(index, d * count, a_v, at_row, cells_in, 1, rows)
            return carry

        for q in range(GROUPS):
            fetch(q).wait()
            lax.fori_loop(q * some, (q + 1) * some, arrive, 0)
        advect(((0, width),), coefs, picks, cells_in, cells_out, levels)
        mine = place[0] * count + at
        for u0 in range(0, width, BATCH):
            own = [pl.ds(index[mine + u], 1) for u in range(u0, u0 + BATCH)]
            sums = [cells_out[own[u], :] + extra[u0 + u : u0 + u + 1, :] for u in range(BATCH)]
            for u in range(BATCH):
                cells_out[own[u], :] = sums[u]

        def pick(c, slot):
            gather_rows(index, c * LANES, cells_out, tiles[slot], 1, LANES)

        def turn(c, slot):
            at_lane = pl.multiple_of(c * LANES, LANES)
            o_v[:, pl.ds(at_lane, LANES)] = tiles[slot][0:LANES, :].T[:width]

        wide = CELLS // GROUPS
        each = wide // LANES

        def send(q):
            part = pl.ds(q * wide, wide)
            return pltpu.make_async_copy(o_v.at[:, part], o_hbm.at[pl.ds(at, width), part], sem_out.at[q])

        pick(0, 0)

        def body(b, carry):
            c = 2 * b
            pick(c + 1, 1)
            turn(c, 0)
            pick(jnp.minimum(c + 2, CELLS // LANES - 1), 0)
            turn(c + 1, 1)
            return carry

        for q in range(GROUPS):
            lax.fori_loop(q * each // 2, (q + 1) * each // 2, body, 0)
            send(q).start()
        for q in range(GROUPS):
            send(q).wait()

    return kernel


def shards(covariance, advective_ratio, flow_heading_flags, cell_of_state, added_uncertainty):
    count = covariance.shape[0]
    devices = lax.axis_size(AXES)
    here = lax.axis_index(AXES)
    smem = pl.BlockSpec(memory_space=pltpu.SMEM)
    vmem = pl.BlockSpec(memory_space=pltpu.VMEM)
    hbm = pl.BlockSpec(memory_space=pl.ANY)
    f32 = jnp.float32
    slots = len(spans_first(count))
    cells = (slots * CELLS, LANES)
    sems = pltpu.SemaphoreType.DMA((GROUPS,))

    def levels(rows):
        return [pltpu.VMEM((RING, rows, LON), f32)] * (ADVECTION_TOTAL + 1)

    def tiles(rows):
        return [pltpu.VMEM((rows, LANES), f32)] * 2

    def params(mib):
        return pltpu.CompilerParams(vmem_limit_bytes=mib * MIB)

    def cost(us):
        return pl.CostEstimate(flops=us * 10**6, bytes_accessed=us * 3 * 10**6, transcendentals=0)

    own = advective_ratio[0].reshape(1, ADVECTION_TOTAL * 2, count)
    spread = jnp.broadcast_to(own, (devices, ADVECTION_TOTAL * 2, count))
    rates = lax.all_to_all(spread, AXES, split_axis=0, concat_axis=0, tiled=True)
    rates = jnp.transpose(rates, (1, 0, 2)).reshape(ADVECTION_TOTAL, 2, LAT, LON)
    heading = flow_heading_flags[0].reshape(ADVECTION_TOTAL, 2, LAT, LON)
    rate_x, rate_y = rates[:, 0], rates[:, 1]
    lat = lax.broadcasted_iota(jnp.int32, (ADVECTION_TOTAL, LAT, LON), 1)
    outside = lat == jnp.where(heading[:, 1] == 1, 0, LAT - 1)
    coefs = jnp.stack([1.0 - rate_x - rate_y, rate_x, jnp.where(outside, 0.0, rate_y)], axis=1)
    lane = lax.broadcasted_iota(jnp.int32, (ADVECTION_TOTAL, LAT, LON), 2)
    pick_x = jnp.where(heading[:, 0] == 1, lane + (LON - 1), lane + 1) % LON
    picks = jnp.stack([pick_x, heading[:, 1]], axis=1)

    parts = spans_second(count)
    blocks = [
        (devices, count // 2 if is_packed(count, width) else count, LANES) for _, width in parts
    ]
    moved = []
    for (at, width), shape in zip(parts, blocks):
        staging = [pltpu.VMEM(shape, f32)] + tiles(slots * LANES) + [sems]
        if at == 0:
            sent, advected = pl.pallas_call(
                first_pass(count, at, width),
                out_shape=(jax.ShapeDtypeStruct(shape, f32), jax.ShapeDtypeStruct(cells, f32)),
                in_specs=[smem, hbm, vmem, vmem],
                out_specs=(hbm, hbm),
                scratch_shapes=[pltpu.VMEM(covariance.shape, f32)]
                + [pltpu.VMEM(cells, f32)] * 2
                + staging[:-1]
                + [sems, sems, pltpu.SemaphoreType.DMA(())]
                + levels(count),
                compiler_params=params(60),
                cost_estimate=cost(25),
                name="first_pass",
            )(cell_of_state, covariance, coefs, picks)
        else:
            sent = pl.pallas_call(
                first_rest(count, at, width),
                out_shape=jax.ShapeDtypeStruct(shape, f32),
                in_specs=[smem, vmem],
                out_specs=hbm,
                scratch_shapes=staging,
                compiler_params=params(60),
                cost_estimate=cost(6),
                name="first_rest",
            )(cell_of_state, advected)
        arrived = lax.all_to_all(sent, AXES, split_axis=0, concat_axis=0, tiled=True)
        moved.append(arrived.reshape(devices * shape[1], LANES))

    result = None
    for (at, width), arrived in zip(parts, moved):
        lane = lax.broadcasted_iota(jnp.int32, (width, LANES), 1)
        row = lax.broadcasted_iota(jnp.int32, (width, LANES), 0)
        extra = jnp.where(lane == row, added_uncertainty[0, at : at + width, None], 0.0)
        args = [cell_of_state, here.reshape(1), arrived, coefs, picks, extra]
        specs = [smem, smem, hbm, vmem, vmem, vmem]
        if at:
            args.append(result)
            specs.append(hbm)
        result = pl.pallas_call(
            second_pass(count, devices, at, width),
            out_shape=jax.ShapeDtypeStruct((count, CELLS), f32),
            in_specs=specs,
            out_specs=hbm,
            scratch_shapes=[
                pltpu.VMEM(arrived.shape, f32),
                pltpu.VMEM((CELLS, LANES), f32),
                pltpu.VMEM((CELLS, LANES), f32),
                pltpu.VMEM((width, CELLS), f32),
            ]
            + tiles(LANES)
            + [sems, sems]
            + levels(width),
            input_output_aliases={6: 0} if at else {},
            compiler_params=params(60),
            cost_estimate=cost(25),
            name="second_pass",
        )(*args)
    return result


def solution(mesh):
    in_specs = (
        P(AXES, None),
        P(None, None, None, AXES),
        P(),
        P(),
        P(None, AXES),
    )
    return jax.shard_map(shards, mesh=mesh, in_specs=in_specs, out_specs=P(AXES, None), check_vma=False)
```

time: 1090 us -> 198 us (0.18)
  other arithmetic: 584 us -> 2.91 us
  local copies, waits for them, and re-layouts: 275 us -> 2.76 us
  Pallas kernels: 0 us -> 95.4 us
  blocking collectives: 84.3 us -> 0 us
  waiting for transfers between devices: 139 us -> 82 us
    sub x1, other arithmetic: 267 us -> 0.03 us  [shards(): 1.0 - rate_x - rate_y]
    select_n x4 -> x3, other arithmetic: 217 us -> 1.42 us  [the longest x2 1.37 us: shards(): jnp.where(lane == row, added_uncertainty[0, at:at + width, None], 0.0)]
    slice x24 -> x0, local copies, waits for them, and re-layouts: 117 us -> none  [the longest x16 65.5 us: substep_move(): east_cell = jnp.roll(values, -1, axis=2)]
    gather x4 -> x0, local copies, waits for them, and re-layouts: 108 us -> none  [the longest x2 55 us: apply_rows(): jnp.take(on_grid.reshape(count_rows, LAT * LON), cell_of_state, axis=1)]
    add x10 -> x1, other arithmetic: 98.5 us -> 0.01 us  [shards(): pick_x = jnp.where(heading[:, 0] == 1, lane + (LON - 1), lane + 1) % LON]
    pallas_call x0 -> x4, Pallas kernels: none -> 95.4 us  [the longest x2 56.7 us: shards(): pl.pallas_call(second_pass(count, devices, at, width), out_shape=jax.Shap...]
    all_gather x1 -> x0, blocking collectives: 84.3 us -> none  [shards(): lax.all_gather(advective_ratio[0], ('row', 'col'), axis=2, tiled=True)]
    all_to_all x1 -> x3, waiting for transfers between devices: 139 us -> 82 us  [the longest x2 73.9 us: shards(): lax.all_to_all(sent, AXES, split_axis=0, concat_axis=0, tiled=True)]
  transfers between devices with their start and end apart: 1 -> 3, of which waited for: 1 -> 3; matrix products, arithmetic and copies ran while one was open for 0% -> 2% of each run, Pallas kernels for 0% -> 18%
where the time goes in v2:
time: 198 us; the launch traced here: 197 us
  Pallas kernels  95.4 us (48%)
  waiting for transfers between devices  82 us (41%)
  starting transfers between devices  13.9 us (7%)
  other arithmetic  2.91 us (1%)
  local copies, waits for them, and re-layouts  2.76 us (1%)
    all_to_all x2, waiting for transfers between devices, shards(): lax.all_to_all(sent, AXES, split_axis=0, concat_axis=0, tiled=True)  73.9 us
    pallas_call x2, Pallas kernels, shards(): pl.pallas_call(second_pass(count, devices, at, width), out_shape=jax.Shap...  56.7 us
    pallas_call x1, Pallas kernels, shards(): pl.pallas_call(first_pass(count, at, width), out_shape=(jax.ShapeDtypeStr...  32.5 us
    all_to_all x1, waiting for transfers between devices, shards(): lax.all_to_all(spread, AXES, split_axis=0, concat_axis=0, tiled=True)  8.13 us
    all_to_all x1, starting transfers between devices, shards(): lax.all_to_all(spread, AXES, split_axis=0, concat_axis=0, tiled=True)  7.33 us
    all_to_all x2, starting transfers between devices, shards(): lax.all_to_all(sent, AXES, split_axis=0, concat_axis=0, tiled=True)  6.53 us
    pallas_call x1, Pallas kernels, shards(): pl.pallas_call(first_rest(count, at, width), out_shape=jax.ShapeDtypeStru...  6.26 us
  transfers between devices with their start and end apart: 3, of which 3 were waited for; matrix products, arithmetic and copies ran while one was open for 2% of the time, Pallas kernels for 18%

profile of v2, /device:TPU:0, one launch (start us, length us, event | category | flops | bytes accessed | tf_op | source)
XLA Modules:
  0.0 197.3 jit_solution(6938304484971021486)
XLA Ops:
  0.0 0.7 broadcast_in_dim.47
  0.7 0.7 broadcast_in_dim.48
  1.4 7.3 %all-to-all-start = ((f32[32,8,192]{2,1,0:T(8,128)}), f32[32,8,192]{2,1,0:T(8,128)S(1)}, u32[]{:S(2)}, u32[]{:S(2)}) async-start(f32[32,8,192]{2,1,0:T(8,128)} %broadcast_in_dim.48), calls=%async_computation | async-start | bytes 524288 | tf_op jit(solution)/shard_map/all_to_all | solution.py:308
  8.8 1.1 reshape_squeeze.4
  9.9 0.7 pad_add_fusion.picks
  10.6 8.1 %all-to-all-done = f32[32,8,192]{2,1,0:T(8,128)S(1)} async-done(((f32[32,8,192]{2,1,0:T(8,128)}), f32[32,8,192]{2,1,0:T(8,128)S(1)}, u32[]{:S(2)}, u32[]{:S(2)}) %all-to-all-start) | async-done | bytes 196640 | tf_op jit(solution)/shard_map/all_to_all | solution.py:308
  18.8 0.1 copy.7
  18.9 0.1 reshape.18
  19.0 0.7 pad_maximum_fusion.coefs
  19.8 32.5 %first_pass.1 = (f32[32,192,128]{2,1,0:T(8,128)}, f32[12288,128]{1,0:T(8,128)}) custom-call(s32[6144]{0:T(1024)} %index.7, f32[192,6144]{1,0:T(8,128)} %x_hbm.1, f32[4,3,48,128]{3,2,1,0:T(8,128)} %pad_maximum_fusion.coefs, s32[4,2,48,128]{3,2,1,0:T(8,128)} %pad_add_fusion.picks), custom_call_target="tpu_custom_call" | custom-call | flops 25000000 | bytes 75000000 | tf_op jit(solution)/shard_map/first_pass/pallas_call | solution.py:327
  52.3 2.9 %all-to-all-start.2 = ((f32[32,192,128]{2,1,0:T(8,128)}), f32[32,192,128]{2,1,0:T(8,128)S(1)}, u32[]{:S(2)}, u32[]{:S(2)}) async-start(f32[32,192,128]{2,1,0:T(8,128)} %get-tuple-element.8), calls=%async_computation.2 | async-start | bytes 6291456 | tf_op jit(solution)/shard_map/all_to_all | solution.py:352
  55.2 0.0 copy-start.1
  55.2 6.3 %first_rest.1 = f32[32,96,128]{2,1,0:T(8,128)} custom-call(s32[6144]{0:T(1024)} %index.7, f32[12288,128]{1,0:T(8,128)} %get-tuple-element.7.cells), custom_call_target="tpu_custom_call" | custom-call | flops 6000000 | bytes 18000000 | tf_op jit(solution)/shard_map/first_rest/pallas_call | solution.py:342
  61.5 66.2 %all-to-all-done.2 = f32[32,192,128]{2,1,0:T(8,128)S(1)} async-done(((f32[32,192,128]{2,1,0:T(8,128)}), f32[32,192,128]{2,1,0:T(8,128)S(1)}, u32[]{:S(2)}, u32[]{:S(2)}) %all-to-all-start.2) | async-done | bytes 3145760 | tf_op jit(solution)/shard_map/all_to_all | solution.py:352
  127.7 0.0 copy-start
  127.7 3.7 %all-to-all-start.1 = ((f32[32,96,128]{2,1,0:T(8,128)}), f32[32,96,128]{2,1,0:T(8,128)}, u32[]{:S(2)}, u32[]{:S(2)}) async-start(f32[32,96,128]{2,1,0:T(8,128)} %first_rest.1), calls=%async_computation.1 | async-start | bytes 3145728 | tf_op jit(solution)/shard_map/all_to_all | solution.py:352
  131.4 0.0 copy-done.1
  131.4 0.7 fusion.3.extra
  132.1 0.7 fusion.2.extra
  132.8 0.0 copy-done
  132.8 29.5 %second_pass.2.rest_0_ = f32[192,6144]{1,0:T(8,128)} custom-call(s32[6144]{0:T(1024)} %index.7, s32[1]{0:T(128)} %bitcast.place, f32[6144,128]{1,0:T(8,128)} %bitcast.8, f32[4,3,48,128]{3,2,1,0:T(8,128)} %pad_maximum_fusion.coefs, s32[4,2,48,128]{3,2,1,0:T(8,128)} %pad_add_fusion.picks, f32[128,128]{1,0:T(8,128)} %fusion.2.extra), custom_call_target="tpu_custom_call" | custom-call | flops 25000000 | bytes 75000000 | tf_op jit(solution)/shard_map/second_pass/pallas_call | solution.py:365
  162.3 7.7 %all-to-all-done.1 = f32[32,96,128]{2,1,0:T(8,128)} async-done(((f32[32,96,128]{2,1,0:T(8,128)}), f32[32,96,128]{2,1,0:T(8,128)}, u32[]{:S(2)}, u32[]{:S(2)}) %all-to-all-start.1) | async-done | bytes 1572896 | tf_op jit(solution)/shard_map/all_to_all | solution.py:352
  169.9 27.2 %second_pass.3 = f32[192,6144]{1,0:T(8,128)} custom-call(s32[6144]{0:T(1024)} %index.7, s32[1]{0:T(128)} %bitcast.place, f32[3072,128]{1,0:T(8,128)} %bitcast.2.a_hbm, f32[4,3,48,128]{3,2,1,0:T(8,128)} %pad_maximum_fusion.coefs, s32[4,2,48,128]{3,2,1,0:T(8,128)} %pad_add_fusion.picks, f32[64,128]{1,0:T(8,128)} %fusion.3.extra, ...), custom_call_target="tpu_custom_call", output_to_operand_aliasing={{}: (6, {})} | custom-call | flops 25000000 | bytes 75000000 | tf_op jit(solution)/shard_map/second_pass/pallas_call | solution.py:365
  (5 shorter events, 0.1 us)
Async XLA Ops:
  1.4 17.3 %all-to-all-start = ((f32[32,8,192]{2,1,0:T(8,128)}), f32[32,8,192]{2,1,0:T(8,128)S(1)}, u32[]{:S(2)}, u32[]{:S(2)}) async-start(f32[32,8,192]{2,1,0:T(8,128)} %broadcast_in_dim.48), calls=%async_computation | async-start | bytes 524288 | tf_op jit(solution)/shard_map/all_to_all | solution.py:308
  52.3 75.4 %all-to-all-start.2 = ((f32[32,192,128]{2,1,0:T(8,128)}), f32[32,192,128]{2,1,0:T(8,128)S(1)}, u32[]{:S(2)}, u32[]{:S(2)}) async-start(f32[32,192,128]{2,1,0:T(8,128)} %get-tuple-element.8), calls=%async_computation.2 | async-start | bytes 6291456 | tf_op jit(solution)/shard_map/all_to_all | solution.py:352
  55.2 76.2 %copy-start.1 = (f32[1,192]{1,0:T(1,128)S(1)}, f32[1,192]{1,0:T(1,128)}, u32[]{:S(2)}) copy-start(f32[1,192]{1,0:T(1,128)} %param.9) | copy-start | bytes 2308
  127.7 5.1 %copy-start = (f32[32,192,128]{2,1,0:T(8,128)}, f32[32,192,128]{2,1,0:T(8,128)S(1)}, u32[]{:S(2)}) copy-start(f32[32,192,128]{2,1,0:T(8,128)S(1)} %all-to-all-done.2) | copy-start | bytes 9437188
  127.7 42.2 %all-to-all-start.1 = ((f32[32,96,128]{2,1,0:T(8,128)}), f32[32,96,128]{2,1,0:T(8,128)}, u32[]{:S(2)}, u32[]{:S(2)}) async-start(f32[32,96,128]{2,1,0:T(8,128)} %first_rest.1), calls=%async_computation.1 | async-start | bytes 3145728 | tf_op jit(solution)/shard_map/all_to_all | solution.py:352

commit v3 on v2

--- a/solution.py
+++ b/solution.py
@@ -1,3 +1,5 @@
+import math
+
 import jax
 import jax.numpy as jnp
 from jax import lax
@@ -11,10 +13,10 @@
 CELLS = LAT * LON
 LANES = 128
 AXES = ("row", "col")
-GROUPS = 8
+GROUPS = 4
 BATCH = 16
-LAG = 2
-RING = 8
+BAND = 2
+RING = 4 * BAND
 MIB = 2**20
 
 
@@ -51,22 +53,35 @@
     return pl.ds(start + h, total, stride=slots) if slots > 1 else pl.ds(start, total)
 
 
-def substep(coefs, picks, s, source, target, i):
-    def spread(ref, which):
-        return jnp.broadcast_to(ref[s, which, pl.ds(i, 1), :], (8, LON))
-
-    remain, rate_x, rate_y = (spread(coefs, w) for w in range(3))
-    pick_x, north = (spread(picks, w) for w in range(2))
-    from_south = north == 1
-    south, middle, above = ((i + d) & (RING - 1) for d in (-1, 0, 1))
+def substep(rates, flags, s, source, target, i):
+    def spread(row):
+        return jnp.broadcast_to(row, (8, LON))
+
+    at_lane = pl.multiple_of(i * LON, LON)
+    rate_x = rates[i, 2 * s : 2 * s + 1, :]
+    rate_y = rates[i, 2 * s + 1 : 2 * s + 2, :]
+    remain = spread(1.0 - rate_x - rate_y)
+    lane = lax.broadcasted_iota(jnp.int32, (1, LON), 1)
+    west = flags[0, s, 0:1, pl.ds(at_lane, LON)] == 1
+    pick_x = spread(jnp.where(west, lane + (LON - 1), lane + 1) & (LON - 1))
+    from_south = spread(flags[0, s, 1:2, pl.ds(at_lane, LON)]) == 1
+    inside = [jnp.where(i == edge, 0.0, 1.0) for edge in (0, LAT - 1)]
+    rate_x = spread(rate_x)
+    rate_y = spread(rate_y) * jnp.where(from_south, inside[0], inside[1])
+    south, middle, north = ((i + d) & (RING - 1) for d in (-1, 0, 1))
     for g in range(0, source.shape[1], 8):
         here = source[middle, g : g + 8, :]
         side = jnp.take_along_axis(here, pick_x, axis=1)
-        y_side = jnp.where(from_south, source[south, g : g + 8, :], source[above, g : g + 8, :])
+        y_side = jnp.where(from_south, source[south, g : g + 8, :], source[north, g : g + 8, :])
         target[middle, g : g + 8, :] = remain * here + rate_x * side + rate_y * y_side
 
 
-def advect(spans, coefs, picks, cells_in, cells_out, levels):
+def entering():
+    tail = 2 * ADVECTION_TOTAL + 1
+    return ((0, 2), (2, tail), (tail, LAT // BAND))
+
+
+def advect(spans, rates, flags, cells_in, cells_out, levels, ready=None):
     slots = len(spans)
     count = levels[0].shape[1]
 
@@ -82,38 +97,69 @@
 
     for level in levels[:-1]:
         level[RING - 1] = jnp.zeros((count, LON), jnp.float32)
-    tail = LAG * ADVECTION_TOTAL + 1
-
-    def step(i, guard):
+    tail = 2 * ADVECTION_TOTAL + 1
+    bands = LAT // BAND
+
+    def step(b, guard):
         def run(stage, j):
+            def every():
+                for u in range(BAND):
+                    stage(j * BAND + u)
+
             if guard:
-                pl.when((j >= 0) & (j < LAT))(lambda: stage(j))
+                pl.when((j >= 0) & (j < bands))(every)
             else:
-                stage(j)
-
-        run(leave, i - tail)
+                every()
+
+        run(leave, b - tail)
         for s in reversed(range(ADVECTION_TOTAL)):
-            run(lambda j, s=s: substep(coefs, picks, s, levels[s], levels[s + 1], j), i - LAG * (s + 1))
-        run(enter, i)
-
-    def guarded(i, carry):
-        step(i, True)
+            run(lambda i, s=s: substep(rates, flags, s, levels[s], levels[s + 1], i), b - 2 * (s + 1))
+        run(enter, b)
+
+    def guarded(b, carry):
+        step(b, True)
         return carry
 
-    def steady(i, carry):
-        step(i, False)
+    def steady(b, carry):
+        step(b, False)
         return carry
 
-    lax.fori_loop(0, tail, guarded, 0)
-    lax.fori_loop(tail, LAT, steady, 0)
-    lax.fori_loop(LAT, LAT + tail, guarded, 0)
-
-
-def lay_on_grid(index, x_hbm, o_ref, x_v, tiles, sem_in):
+    for q, (start, stop) in enumerate(entering()):
+        if ready is not None:
+            ready(q)
+        lax.fori_loop(start, stop, guarded if start < tail else steady, 0)
+    lax.fori_loop(bands, bands + tail, guarded, 0)
+
+
+def pick_and_turn(pick, turn, send, total):
+    some = total // GROUPS
+    pick(0, 0)
+    pick(1, 1)
+
+    def body(b, carry):
+        i = 4 * b
+        pick(i + 2, 2)
+        pick(i + 3, 3)
+        turn(i, 0)
+        turn(i + 1, 1)
+        pick(jnp.minimum(i + 4, total - 2), 0)
+        pick(jnp.minimum(i + 5, total - 1), 1)
+        turn(i + 2, 2)
+        turn(i + 3, 3)
+        return carry
+
+    for q in range(GROUPS):
+        lax.fori_loop(q * some // 4, (q + 1) * some // 4, body, 0)
+        send(q).start()
+    for q in range(GROUPS):
+        send(q).wait()
+
+
+def lay_on_grid(index, x_hbm, o_hbm, x_v, o_v, tile_a, tile_b, sem_in, sem_out):
     spans = spans_first(x_v.shape[0])
     slots = len(spans)
+    tiles = (tile_a, tile_b)
     wide = CELLS // GROUPS
-    each = wide // LANES
 
     def fetch(q):
         part = pl.ds(q * wide, wide)
@@ -129,7 +175,7 @@
             tiles[slot][slot_rows(0, h, LANES, slots), 0:width] = block.T
 
     def place(c, slot):
-        scatter_rows(index, c * LANES, tiles[slot], 0, o_ref, slots, LANES)
+        scatter_rows(index, c * LANES, tiles[slot], 0, o_v, slots, LANES)
 
     fetch(0).wait()
     turn(0, 0)
@@ -142,10 +188,22 @@
         place(c + 1, 1)
         return carry
 
+    each = wide // LANES // 2
     for q in range(GROUPS):
         if q + 1 < GROUPS:
             fetch(q + 1).wait()
-        lax.fori_loop(q * each // 2, (q + 1) * each // 2, body, 0)
+        lax.fori_loop(q * each, (q + 1) * each, body, 0)
+    out = pltpu.make_async_copy(o_v, o_hbm, sem_out)
+    out.start()
+    out.wait()
+
+
+def gather_rates(shared, rates, count):
+    rates[...] = jnp.zeros_like(rates)
+    for d in range(shared.shape[0]):
+        for t in range(shared.shape[1]):
+            lat = d * count // LANES + t
+            rates[lat] = rates[lat] + shared[d, t]
 
 
 def send_part(index, cells, o_v, o_hbm, tiles, sem_out, count, at, width):
@@ -170,28 +228,23 @@
         part = pl.ds(q * some, some)
         return pltpu.make_async_copy(o_v.at[part], o_hbm.at[part], sem_out.at[q])
 
-    pick(0, 0)
-
-    def body(b, carry):
-        e = 2 * b
-        pick(e + 1, 1)
-        turn(e, 0)
-        pick(jnp.minimum(e + 2, devices - 1), 0)
-        turn(e + 1, 1)
-        return carry
-
-    for q in range(GROUPS):
-        lax.fori_loop(q * some // 2, (q + 1) * some // 2, body, 0)
-        send(q).start()
-    for q in range(GROUPS):
-        send(q).wait()
+    pick_and_turn(pick, turn, send, devices)
 
 
 def first_pass(count, at, width):
-    def kernel(index, x_hbm, coefs, picks, o_hbm, keep_hbm, x_v, cells_in, cells_out, o_v, tile_a, tile_b, sem_in, sem_out, sem_keep, *levels):
-        tiles = (tile_a, tile_b)
-        lay_on_grid(index, x_hbm, cells_in, x_v, tiles, sem_in)
-        advect(spans_first(count), coefs, picks, cells_in, cells_out, levels)
+    def kernel(index, cells_hbm, shared, flags, o_hbm, keep_hbm, rates, cells_in, cells_out, o_v, *rest):
+        tiles, (sem_out, sem_in, sem_keep), levels = rest[:4], rest[4:7], rest[7:]
+        spans = spans_first(count)
+
+        def fetch(q):
+            start, stop = (len(spans) * LON * BAND * b for b in entering()[q])
+            part = pl.ds(start, stop - start)
+            return pltpu.make_async_copy(cells_hbm.at[part], cells_in.at[part], sem_in.at[q])
+
+        for q in range(len(entering())):
+            fetch(q).start()
+        gather_rates(shared, rates, count)
+        advect(spans, rates, flags, cells_in, cells_out, levels, lambda q: fetch(q).wait())
         keep = pltpu.make_async_copy(cells_out, keep_hbm, sem_keep)
         keep.start()
         send_part(index, cells_out, o_v, o_hbm, tiles, sem_out, count, at, width)
@@ -201,8 +254,8 @@
 
 
 def first_rest(count, at, width):
-    def kernel(index, cells, o_hbm, o_v, tile_a, tile_b, sem_out):
-        send_part(index, cells, o_v, o_hbm, (tile_a, tile_b), sem_out, count, at, width)
+    def kernel(index, cells, o_hbm, o_v, *rest):
+        send_part(index, cells, o_v, o_hbm, rest[:4], rest[4], count, at, width)
 
     return kernel
 
@@ -211,11 +264,12 @@
     packed = is_packed(count, width)
     rows = count // 2 if packed else count
 
-    def kernel(index, place, a_hbm, coefs, picks, extra, *rest):
+    def kernel(index, place, a_hbm, rates, flags, extra, *rest):
         if at:
             rest = rest[1:]
-        o_hbm, a_v, cells_in, cells_out, o_v, tile_a, tile_b, sem_in, sem_out, *levels = rest
-        tiles = (tile_a, tile_b)
+        o_hbm, a_v, cells_in, cells_out, o_v, *rest = rest
+        tiles, (sem_in, sem_out), levels = rest[:4], rest[4:6], rest[6:]
+        tile_a = tiles[0]
         some = devices // GROUPS
 
         def fetch(q):
@@ -238,7 +292,7 @@
         for q in range(GROUPS):
             fetch(q).wait()
             lax.fori_loop(q * some, (q + 1) * some, arrive, 0)
-        advect(((0, width),), coefs, picks, cells_in, cells_out, levels)
+        advect(((0, width),), rates, flags, cells_in, cells_out, levels)
         mine = place[0] * count + at
         for u0 in range(0, width, BATCH):
             own = [pl.ds(index[mine + u], 1) for u in range(u0, u0 + BATCH)]
@@ -254,27 +308,12 @@
             o_v[:, pl.ds(at_lane, LANES)] = tiles[slot][0:LANES, :].T[:width]
 
         wide = CELLS // GROUPS
-        each = wide // LANES
 
         def send(q):
             part = pl.ds(q * wide, wide)
             return pltpu.make_async_copy(o_v.at[:, part], o_hbm.at[pl.ds(at, width), part], sem_out.at[q])
 
-        pick(0, 0)
-
-        def body(b, carry):
-            c = 2 * b
-            pick(c + 1, 1)
-            turn(c, 0)
-            pick(jnp.minimum(c + 2, CELLS // LANES - 1), 0)
-            turn(c + 1, 1)
-            return carry
-
-        for q in range(GROUPS):
-            lax.fori_loop(q * each // 2, (q + 1) * each // 2, body, 0)
-            send(q).start()
-        for q in range(GROUPS):
-            send(q).wait()
+        pick_and_turn(pick, turn, send, CELLS // LANES)
 
     return kernel
 
@@ -295,7 +334,7 @@
         return [pltpu.VMEM((RING, rows, LON), f32)] * (ADVECTION_TOTAL + 1)
 
     def tiles(rows):
-        return [pltpu.VMEM((rows, LANES), f32)] * 2
+        return [pltpu.VMEM((rows, LANES), f32)] * 4
 
     def params(mib):
         return pltpu.CompilerParams(vmem_limit_bytes=mib * MIB)
@@ -303,18 +342,27 @@
     def cost(us):
         return pl.CostEstimate(flops=us * 10**6, bytes_accessed=us * 3 * 10**6, transcendentals=0)
 
-    own = advective_ratio[0].reshape(1, ADVECTION_TOTAL * 2, count)
-    spread = jnp.broadcast_to(own, (devices, ADVECTION_TOTAL * 2, count))
-    rates = lax.all_to_all(spread, AXES, split_axis=0, concat_axis=0, tiled=True)
-    rates = jnp.transpose(rates, (1, 0, 2)).reshape(ADVECTION_TOTAL, 2, LAT, LON)
-    heading = flow_heading_flags[0].reshape(ADVECTION_TOTAL, 2, LAT, LON)
-    rate_x, rate_y = rates[:, 0], rates[:, 1]
-    lat = lax.broadcasted_iota(jnp.int32, (ADVECTION_TOTAL, LAT, LON), 1)
-    outside = lat == jnp.where(heading[:, 1] == 1, 0, LAT - 1)
-    coefs = jnp.stack([1.0 - rate_x - rate_y, rate_x, jnp.where(outside, 0.0, rate_y)], axis=1)
-    lane = lax.broadcasted_iota(jnp.int32, (ADVECTION_TOTAL, LAT, LON), 2)
-    pick_x = jnp.where(heading[:, 0] == 1, lane + (LON - 1), lane + 1) % LON
-    picks = jnp.stack([pick_x, heading[:, 1]], axis=1)
+    own = advective_ratio[0].reshape(ADVECTION_TOTAL * 2, count)
+    held = -(-(count + LANES - math.gcd(count, LANES)) // LANES)
+    own = lax.dynamic_update_slice(
+        jnp.zeros((ADVECTION_TOTAL * 2, held * LANES), f32), own, (0, count * here % LANES)
+    )
+    own = jnp.transpose(own.reshape(ADVECTION_TOTAL * 2, held, LANES), (1, 0, 2))
+    own = jnp.broadcast_to(own[None], (devices,) + own.shape)
+    shared = lax.all_to_all(own, AXES, split_axis=0, concat_axis=0, tiled=True)
+
+    on_grid = pl.pallas_call(
+        lay_on_grid,
+        out_shape=jax.ShapeDtypeStruct(cells, f32),
+        in_specs=[smem, hbm],
+        out_specs=hbm,
+        scratch_shapes=[pltpu.VMEM(covariance.shape, f32), pltpu.VMEM(cells, f32)]
+        + tiles(slots * LANES)[:2]
+        + [sems, pltpu.SemaphoreType.DMA(())],
+        compiler_params=params(60),
+        cost_estimate=cost(10),
+        name="lay_on_grid",
+    )(cell_of_state, covariance)
 
     parts = spans_second(count)
     blocks = [
@@ -324,20 +372,23 @@
     for (at, width), shape in zip(parts, blocks):
         staging = [pltpu.VMEM(shape, f32)] + tiles(slots * LANES) + [sems]
         if at == 0:
-            sent, advected = pl.pallas_call(
+            sent, advected, rates = pl.pallas_call(
                 first_pass(count, at, width),
-                out_shape=(jax.ShapeDtypeStruct(shape, f32), jax.ShapeDtypeStruct(cells, f32)),
+                out_shape=(
+                    jax.ShapeDtypeStruct(shape, f32),
+                    jax.ShapeDtypeStruct(cells, f32),
+                    jax.ShapeDtypeStruct((LAT + held, ADVECTION_TOTAL * 2, LON), f32),
+                ),
                 in_specs=[smem, hbm, vmem, vmem],
-                out_specs=(hbm, hbm),
-                scratch_shapes=[pltpu.VMEM(covariance.shape, f32)]
-                + [pltpu.VMEM(cells, f32)] * 2
-                + staging[:-1]
-                + [sems, sems, pltpu.SemaphoreType.DMA(())]
+                out_specs=(hbm, hbm, vmem),
+                scratch_shapes=[pltpu.VMEM(cells, f32)] * 2
+                + staging
+                + [sems, pltpu.SemaphoreType.DMA(())]
                 + levels(count),
                 compiler_params=params(60),
                 cost_estimate=cost(25),
                 name="first_pass",
-            )(cell_of_state, covariance, coefs, picks)
+            )(cell_of_state, on_grid, shared, flow_heading_flags)
         else:
             sent = pl.pallas_call(
                 first_rest(count, at, width),
@@ -357,7 +408,7 @@
         lane = lax.broadcasted_iota(jnp.int32, (width, LANES), 1)
         row = lax.broadcasted_iota(jnp.int32, (width, LANES), 0)
         extra = jnp.where(lane == row, added_uncertainty[0, at : at + width, None], 0.0)
-        args = [cell_of_state, here.reshape(1), arrived, coefs, picks, extra]
+        args = [cell_of_state, here.reshape(1), arrived, rates, flow_heading_flags, extra]
         specs = [smem, smem, hbm, vmem, vmem, vmem]
         if at:
             args.append(result)

time: 198 us -> 191 us (0.965)
  waiting for transfers between devices: 82 us -> 76 us
  starting transfers between devices: 13.9 us -> 16.8 us
    pallas_call x0 -> x1, Pallas kernels: none -> 12.1 us  [shards(): pl.pallas_call(lay_on_grid, out_shape=jax.ShapeDtypeStruct(cells, f32), i...]
    pallas_call x1, Pallas kernels: 32.5 us -> 24.3 us  [shards(): pl.pallas_call(first_pass(count, at, width), out_shape=(jax.ShapeDtypeStr...]
    all_to_all x1, waiting for transfers between devices: 8.13 us -> 0.01 us  [shards(): shared = lax.all_to_all(own, AXES, split_axis=0, concat_axis=0, tiled=True)]
    pallas_call x2, Pallas kernels: 56.7 us -> 50.6 us  [shards(): pl.pallas_call(second_pass(count, devices, at, width), out_shape=jax.Shap...]
    all_to_all x2, starting transfers between devices: 6.53 us -> 9.5 us  [shards(): lax.all_to_all(sent, AXES, split_axis=0, concat_axis=0, tiled=True)]
    all_to_all x2, waiting for transfers between devices: 73.9 us -> 76 us  [shards(): lax.all_to_all(sent, AXES, split_axis=0, concat_axis=0, tiled=True)]
  transfers between devices with their start and end apart: 3 -> 3, of which waited for: 3 -> 2; matrix products, arithmetic and copies ran while one was open for 2% -> 1% of each run, Pallas kernels for 18% -> 24%
where the time goes in v3:
time: 191 us
  Pallas kernels  93.7 us (49%)
  waiting for transfers between devices  76 us (40%)
  starting transfers between devices  16.8 us (9%)
  local copies, waits for them, and re-layouts  2.35 us (1%)
    all_to_all x2, waiting for transfers between devices, shards(): lax.all_to_all(sent, AXES, split_axis=0, concat_axis=0, tiled=True)  76 us
    pallas_call x2, Pallas kernels, shards(): pl.pallas_call(second_pass(count, devices, at, width), out_shape=jax.Shap...  50.6 us
    pallas_call x1, Pallas kernels, shards(): pl.pallas_call(first_pass(count, at, width), out_shape=(jax.ShapeDtypeStr...  24.3 us
    pallas_call x1, Pallas kernels, shards(): pl.pallas_call(lay_on_grid, out_shape=jax.ShapeDtypeStruct(cells, f32), i...  12.1 us
    all_to_all x2, starting transfers between devices, shards(): lax.all_to_all(sent, AXES, split_axis=0, concat_axis=0, tiled=True)  9.5 us
    all_to_all x1, starting transfers between devices, shards(): shared = lax.all_to_all(own, AXES, split_axis=0, concat_axis=0, tiled=True)  7.33 us
    pallas_call x1, Pallas kernels, shards(): pl.pallas_call(first_rest(count, at, width), out_shape=jax.ShapeDtypeStru...  6.7 us
  transfers between devices with their start and end apart: 3, of which 2 were waited for; matrix products, arithmetic and copies ran while one was open for 1% of the time, Pallas kernels for 24%

profile of v3, /device:TPU:0, one launch (start us, length us, event | category | flops | bytes accessed | tf_op | source)
XLA Modules:
  0.0 190.6 jit_solution(7130106407295973377)
XLA Ops:
  0.0 0.7 reshape_squeeze.3
  0.7 0.2 dynamic_update_slice.3
  0.9 0.7 broadcast_in_dim.38
  1.7 7.3 %all-to-all-start = ((f32[32,2,8,128]{3,2,1,0:T(8,128)}), f32[32,2,8,128]{3,2,1,0:T(8,128)S(1)}, u32[]{:S(2)}, u32[]{:S(2)}) async-start(f32[32,2,8,128]{3,2,1,0:T(8,128)} %broadcast_in_dim.38), calls=%async_computation | async-start | bytes 524288 | tf_op jit(solution)/shard_map/all_to_all | solution.py:352
  9.0 12.1 %lay_on_grid.1.cells_hbm = f32[12288,128]{1,0:T(8,128)} custom-call(s32[6144]{0:T(1024)} %index.9, f32[192,6144]{1,0:T(8,128)} %x_hbm.1), custom_call_target="tpu_custom_call" | custom-call | flops 10000000 | bytes 30000000 | tf_op jit(solution)/shard_map/lay_on_grid/pallas_call | solution.py:354
  21.1 0.0 all-to-all-done.shared
  21.1 0.0 copy-start.1
  21.1 0.7 copy-done.1
  21.8 24.3 %first_pass.1 = (f32[32,192,128]{2,1,0:T(8,128)}, f32[12288,128]{1,0:T(8,128)}, f32[50,8,128]{2,1,0:T(8,128)}) custom-call(s32[6144]{0:T(1024)} %index.9, f32[12288,128]{1,0:T(8,128)} %lay_on_grid.1.cells_hbm, f32[32,2,8,128]{3,2,1,0:T(8,128)} %copy-done.1, s32[1,4,2,6144]{3,2,1,0:T(2,128)} %flags.5), custom_call_target="tpu_custom_call" | custom-call | flops 25000000 | bytes 75000000 | tf_op jit(solution)/shard_map/first_pass/pallas_call | solution.py:375
  46.1 5.8 %all-to-all-start.2 = ((f32[32,192,128]{2,1,0:T(8,128)}), f32[32,192,128]{2,1,0:T(8,128)S(1)}, u32[]{:S(2)}, u32[]{:S(2)}) async-start(f32[32,192,128]{2,1,0:T(8,128)} %get-tuple-element.10), calls=%async_computation.2 | async-start | bytes 6291456 | tf_op jit(solution)/shard_map/all_to_all | solution.py:403
  52.0 0.0 copy-start.2
  52.0 6.7 %first_rest.1 = f32[32,96,128]{2,1,0:T(8,128)} custom-call(s32[6144]{0:T(1024)} %index.9, f32[12288,128]{1,0:T(8,128)} %get-tuple-element.8.cells), custom_call_target="tpu_custom_call" | custom-call | flops 6000000 | bytes 18000000 | tf_op jit(solution)/shard_map/first_rest/pallas_call | solution.py:393
  58.7 65.8 %all-to-all-done.2 = f32[32,192,128]{2,1,0:T(8,128)S(1)} async-done(((f32[32,192,128]{2,1,0:T(8,128)}), f32[32,192,128]{2,1,0:T(8,128)S(1)}, u32[]{:S(2)}, u32[]{:S(2)}) %all-to-all-start.2) | async-done | bytes 3145760 | tf_op jit(solution)/shard_map/all_to_all | solution.py:403
  124.5 0.0 copy-start
  124.5 3.7 %all-to-all-start.1 = ((f32[32,96,128]{2,1,0:T(8,128)}), f32[32,96,128]{2,1,0:T(8,128)}, u32[]{:S(2)}, u32[]{:S(2)}) async-start(f32[32,96,128]{2,1,0:T(8,128)} %first_rest.1), calls=%async_computation.1 | async-start | bytes 3145728 | tf_op jit(solution)/shard_map/all_to_all | solution.py:403
  128.1 0.0 copy-done.2
  128.2 0.7 fusion.1.extra
  128.9 0.7 fusion.extra
  129.6 0.0 copy-done
  129.6 26.9 %second_pass.2.rest_0_ = f32[192,6144]{1,0:T(8,128)} custom-call(s32[6144]{0:T(1024)} %index.9, s32[1]{0:T(128)} %bitcast.place, f32[6144,128]{1,0:T(8,128)} %bitcast.10, f32[50,8,128]{2,1,0:T(8,128)} %get-tuple-element.9.rates, s32[1,4,2,6144]{3,2,1,0:T(2,128)} %flags.5, f32[128,128]{1,0:T(8,128)} %fusion.extra), custom_call_target="tpu_custom_call" | custom-call | flops 25000000 | bytes 75000000 | tf_op jit(solution)/shard_map/second_pass/pallas_call | solution.py:416
  156.5 10.2 %all-to-all-done.1 = f32[32,96,128]{2,1,0:T(8,128)} async-done(((f32[32,96,128]{2,1,0:T(8,128)}), f32[32,96,128]{2,1,0:T(8,128)}, u32[]{:S(2)}, u32[]{:S(2)}) %all-to-all-start.1) | async-done | bytes 1572896 | tf_op jit(solution)/shard_map/all_to_all | solution.py:403
  166.7 23.7 %second_pass.3 = f32[192,6144]{1,0:T(8,128)} custom-call(s32[6144]{0:T(1024)} %index.9, s32[1]{0:T(128)} %bitcast.place, f32[3072,128]{1,0:T(8,128)} %bitcast.3.a_hbm, f32[50,8,128]{2,1,0:T(8,128)} %get-tuple-element.9.rates, s32[1,4,2,6144]{3,2,1,0:T(2,128)} %flags.5, f32[64,128]{1,0:T(8,128)} %fusion.1.extra, ...), custom_call_target="tpu_custom_call", output_to_operand_aliasing={{}: (6, {})} | custom-call | flops 25000000 | bytes 75000000 | tf_op jit(solution)/shard_map/second_pass/pallas_call | solution.py:416
  (3 shorter events, 0.0 us)
Async XLA Ops:
  1.7 19.4 %all-to-all-start = ((f32[32,2,8,128]{3,2,1,0:T(8,128)}), f32[32,2,8,128]{3,2,1,0:T(8,128)S(1)}, u32[]{:S(2)}, u32[]{:S(2)}) async-start(f32[32,2,8,128]{3,2,1,0:T(8,128)} %broadcast_in_dim.38), calls=%async_computation | async-start | bytes 524288 | tf_op jit(solution)/shard_map/all_to_all | solution.py:352
  21.1 0.7 copy-start.1
  46.1 78.4 %all-to-all-start.2 = ((f32[32,192,128]{2,1,0:T(8,128)}), f32[32,192,128]{2,1,0:T(8,128)S(1)}, u32[]{:S(2)}, u32[]{:S(2)}) async-start(f32[32,192,128]{2,1,0:T(8,128)} %get-tuple-element.10), calls=%async_computation.2 | async-start | bytes 6291456 | tf_op jit(solution)/shard_map/all_to_all | solution.py:403
  52.0 76.2 %copy-start.2 = (f32[1,192]{1,0:T(1,128)S(1)}, f32[1,192]{1,0:T(1,128)}, u32[]{:S(2)}) copy-start(f32[1,192]{1,0:T(1,128)} %param.9) | copy-start | bytes 2308
  124.5 5.1 %copy-start = (f32[32,192,128]{2,1,0:T(8,128)}, f32[32,192,128]{2,1,0:T(8,128)S(1)}, u32[]{:S(2)}) copy-start(f32[32,192,128]{2,1,0:T(8,128)S(1)} %all-to-all-done.2) | copy-start | bytes 9437188
  124.5 42.2 %all-to-all-start.1 = ((f32[32,96,128]{2,1,0:T(8,128)}), f32[32,96,128]{2,1,0:T(8,128)}, u32[]{:S(2)}, u32[]{:S(2)}) async-start(f32[32,96,128]{2,1,0:T(8,128)} %first_rest.1), calls=%async_computation.1 | async-start | bytes 3145728 | tf_op jit(solution)/shard_map/all_to_all | solution.py:403

commit v4 on v3

v4 whole, which is shorter than its diff:
```python
import math

import jax
import jax.numpy as jnp
from jax import lax
from jax.experimental import pallas as pl
from jax.experimental.pallas import tpu as pltpu
from jax.sharding import PartitionSpec as P

LAT = 48
LON = 128
ADVECTION_TOTAL = 4
CELLS = LAT * LON
LANES = 128
AXES = ("row", "col")
GROUPS = 4
BATCH = 16
BAND = 2
RING = 4 * BAND
PICKED = 2 * BAND
MIB = 2**20


def spans_first(count):
    half = count // 2
    return ((0, half), (half, half))


def spans_second(count):
    return tuple((at, min(LANES, count - at)) for at in range(0, count, LANES))


def is_packed(count, width):
    return 2 * width == LANES and count > width


def block_rows(count):
    return sum(count // 2 if is_packed(count, width) else count for _, width in spans_second(count))


def slot_rows(start, h, total, slots):
    return pl.ds(start + h, total, stride=slots) if slots > 1 else pl.ds(start, total)


def gather_rows(index, start, source, target, slots, total):
    for u0 in range(0, total, BATCH):
        some = range(u0, min(u0 + BATCH, total))
        rows = [source[pl.ds(pl.multiple_of(slots * index[start + u], slots), slots), :] for u in some]
        for u, row in zip(some, rows):
            target[slots * u : slots * (u + 1), :] = row


def substep(rates, flags, s, source, target, i):
    def spread(row):
        return jnp.broadcast_to(row, (8, LON))

    at_lane = pl.multiple_of(i * LON, LON)
    rate_x = rates[i, 2 * s : 2 * s + 1, :]
    rate_y = rates[i, 2 * s + 1 : 2 * s + 2, :]
    remain = spread(1.0 - rate_x - rate_y)
    lane = lax.broadcasted_iota(jnp.int32, (1, LON), 1)
    west = flags[0, s, 0:1, pl.ds(at_lane, LON)] == 1
    pick_x = spread(jnp.where(west, lane + (LON - 1), lane + 1) & (LON - 1))
    from_south = spread(flags[0, s, 1:2, pl.ds(at_lane, LON)]) == 1
    inside = [jnp.where(i == edge, 0.0, 1.0) for edge in (0, LAT - 1)]
    rate_x = spread(rate_x)
    rate_y = spread(rate_y) * jnp.where(from_south, inside[0], inside[1])
    south, middle, north = ((i + d) & (RING - 1) for d in (-1, 0, 1))
    for g in range(0, source.shape[1], 8):
        here = source[middle, g : g + 8, :]
        side = jnp.take_along_axis(here, pick_x, axis=1)
        y_side = jnp.where(from_south, source[south, g : g + 8, :], source[north, g : g + 8, :])
        target[middle, g : g + 8, :] = remain * here + rate_x * side + rate_y * y_side


def advect(spans, state_of_cell, rates, flags, states_in, cells_out, picked, levels):
    slots = len(spans)
    count = levels[0].shape[1]
    bands = LAT // BAND
    tail = 2 * ADVECTION_TOTAL + 1

    def pick(i):
        gather_rows(state_of_cell, i * LON, states_in, picked.at[i & (PICKED - 1)], slots, LON)

    def enter(i):
        for h, (at, width) in enumerate(spans):
            block = picked.at[i & (PICKED - 1)][slot_rows(0, h, LON, slots), :]
            levels[0][i & (RING - 1), at : at + width, :] = block.T[:width]

    def leave(i):
        for h, (at, width) in enumerate(spans):
            block = levels[-1][i & (RING - 1), at : at + width, :]
            cells_out[slot_rows(slots * LON * i, h, LON, slots), 0:width] = block.T

    def step(b, guard):
        def run(stage, j):
            def every():
                for u in range(BAND):
                    stage(j * BAND + u)

            if guard:
                pl.when((j >= 0) & (j < bands))(every)
            else:
                every()

        run(leave, b - tail)
        for s in reversed(range(ADVECTION_TOTAL)):
            run(lambda i, s=s: substep(rates, flags, s, levels[s], levels[s + 1], i), b - 2 * (s + 1))
        run(enter, b)
        run(pick, b + 1 if guard else jnp.minimum(b + 1, bands - 1))

    def guarded(b, carry):
        step(b, True)
        return carry

    def steady(b, carry):
        step(b, False)
        return carry

    for level in levels[:-1]:
        level[RING - 1] = jnp.zeros((count, LON), jnp.float32)
    lax.fori_loop(-1, tail, guarded, 0)
    lax.fori_loop(tail, bands, steady, 0)
    lax.fori_loop(bands, bands + tail, guarded, 0)


def pick_and_turn(pick, turn, send, total):
    some = total // GROUPS
    pick(0, 0)
    pick(1, 1)

    def body(b, carry):
        i = 4 * b
        pick(i + 2, 2)
        pick(i + 3, 3)
        turn(i, 0)
        turn(i + 1, 1)
        pick(jnp.minimum(i + 4, total - 2), 0)
        pick(jnp.minimum(i + 5, total - 1), 1)
        turn(i + 2, 2)
        turn(i + 3, 3)
        return carry

    for q in range(GROUPS):
        lax.fori_loop(q * some // 4, (q + 1) * some // 4, body, 0)
        send(q).start()
    for q in range(GROUPS):
        send(q).wait()


def turn_rows(cell_of_state, x_hbm, o_hbm, state_of_cell, x_v, o_v, sem_in, sem_out):
    spans = spans_first(x_v.shape[0])
    slots = len(spans)
    wide = CELLS // GROUPS

    def fetch(q):
        part = pl.ds(q * wide, wide)
        return pltpu.make_async_copy(x_hbm.at[:, part], x_v.at[:, part], sem_in.at[q])

    def send(q):
        part = pl.ds(q * slots * wide, slots * wide)
        return pltpu.make_async_copy(o_v.at[part], o_hbm.at[part], sem_out.at[q])

    for q in range(GROUPS):
        fetch(q).start()

    def body(b, carry):
        for c in (2 * b, 2 * b + 1):
            at_lane = pl.multiple_of(c * LANES, LANES)
            for h, (at, width) in enumerate(spans):
                block = x_v[at : at + width, pl.ds(at_lane, LANES)]
                o_v[slot_rows(slots * LANES * c, h, LANES, slots), 0:width] = block.T
            for u in range(LANES):
                state_of_cell[cell_of_state[at_lane + u]] = at_lane + u
        return carry

    each = wide // LANES // 2
    for q in range(GROUPS):
        fetch(q).wait()
        lax.fori_loop(q * each, (q + 1) * each, body, 0)
        send(q).start()
    for q in range(GROUPS):
        send(q).wait()


def gather_rates(shared, rates, count):
    rates[...] = jnp.zeros_like(rates)
    for d in range(shared.shape[0]):
        for t in range(shared.shape[1]):
            lat = d * count // LANES + t
            rates[lat] = rates[lat] + shared[d, t]


def first_pass(
    cell_of_state, state_of_cell, states_hbm, shared, flags, o_hbm, rates, states, cells, o_v, picked, *rest
):
    tiles, (sem_in, sem_out), levels = rest[:4], rest[4:6], rest[6:]
    count = levels[0].shape[1]
    devices = o_v.shape[0]
    spans = spans_first(count)
    slots = len(spans)
    half = count // 2
    rows = slots * CELLS // GROUPS

    def fetch(q):
        part = pl.ds(q * rows, rows)
        return pltpu.make_async_copy(states_hbm.at[part], states.at[part], sem_in.at[q])

    for q in range(GROUPS):
        fetch(q).start()
    gather_rates(shared, rates, count)
    for q in range(GROUPS):
        fetch(q).wait()
    advect(spans, state_of_cell, rates, flags, states, cells, picked, levels)

    def pick(e, slot):
        gather_rows(cell_of_state, e * count, cells, tiles[slot], slots, count)

    def turn(e, slot):
        base = 0
        for at, width in spans_second(count):
            parts = [tiles[slot][slot_rows(slots * at, h, width, slots), :] for h in range(slots)]
            if is_packed(count, width):
                o_v[e, base : base + half, :] = jnp.concatenate(parts, axis=0).T[:half]
                base += half
            else:
                for h in range(slots):
                    o_v[e, base : base + half, 0:width] = parts[h].T[:half]
                    base += half

    some = devices // GROUPS

    def send(q):
        part = pl.ds(q * some, some)
        return pltpu.make_async_copy(o_v.at[part], o_hbm.at[part], sem_out.at[q])

    pick_and_turn(pick, turn, send, devices)


def second_pass(
    cell_of_state, state_of_cell, place, a_hbm, rates, flags, extra, o_hbm, states, cells, o_v, picked, *rest
):
    tiles, (sem_in, sem_out, arrived), levels = rest[:4], rest[4:7], rest[7:]
    count = levels[0].shape[1]
    spans = spans_second(count)
    slots = len(spans)
    half = count // 2

    def unpack(d, carry):
        base = 0
        for h, (_, width) in enumerate(spans):
            start = slots * count * d
            if is_packed(count, width):
                both = arrived[d, base : base + half, :]
                states[slot_rows(start, h, half, slots), :] = both
                states[slot_rows(start + slots * half, h, half, slots), :] = pltpu.roll(both, LANES // 2, 1)
                base += half
            else:
                states[slot_rows(start, h, count, slots), :] = arrived[d, base : base + count, :]
                base += count
        return carry

    some = arrived.shape[0] // GROUPS

    def fetch(q):
        part = pl.ds(q * some, some)
        return pltpu.make_async_copy(a_hbm.at[part], arrived.at[part], sem_in.at[q])

    for q in range(GROUPS):
        fetch(q).start()
    for q in range(GROUPS):
        fetch(q).wait()
        lax.fori_loop(q * some, (q + 1) * some, unpack, 0)
    advect(spans, state_of_cell, rates, flags, states, cells, picked, levels)
    mine = place[0] * count
    for u0 in range(0, count, BATCH):
        own = [pl.ds(slots * cell_of_state[mine + u] + u // LANES, 1) for u in range(u0, u0 + BATCH)]
        sums = [cells[own[u], :] + extra[u0 + u : u0 + u + 1, :] for u in range(BATCH)]
        for u in range(BATCH):
            cells[own[u], :] = sums[u]

    def pick(c, slot):
        gather_rows(cell_of_state, c * LANES, cells, tiles[slot], slots, LANES)

    def turn(c, slot):
        at_lane = pl.multiple_of(c * LANES, LANES)
        for h, (at, width) in enumerate(spans):
            o_v[at : at + width, pl.ds(at_lane, LANES)] = tiles[slot][slot_rows(0, h, LANES, slots), :].T[:width]

    wide = CELLS // GROUPS

    def send(q):
        part = pl.ds(q * wide, wide)
        return pltpu.make_async_copy(o_v.at[:, part], o_hbm.at[:, part], sem_out.at[q])

    pick_and_turn(pick, turn, send, CELLS // LANES)


def shards(covariance, advective_ratio, flow_heading_flags, cell_of_state, added_uncertainty):
    count = covariance.shape[0]
    devices = lax.axis_size(AXES)
    here = lax.axis_index(AXES)
    smem = pl.BlockSpec(memory_space=pltpu.SMEM)
    vmem = pl.BlockSpec(memory_space=pltpu.VMEM)
    hbm = pl.BlockSpec(memory_space=pl.ANY)
    f32 = jnp.float32
    first, second = len(spans_first(count)), len(spans_second(count))
    sems = pltpu.SemaphoreType.DMA((GROUPS,))

    def pass_scratch(slots, picks, out):
        rows = pltpu.VMEM((slots * CELLS, LANES), f32)
        return (
            [rows, rows, pltpu.VMEM(out, f32), pltpu.VMEM((PICKED, slots * LON, LANES), f32)]
            + [pltpu.VMEM((slots * picks, LANES), f32)] * 4
        )

    def params(mib):
        return pltpu.CompilerParams(vmem_limit_bytes=mib * MIB)

    def cost(us):
        return pl.CostEstimate(flops=us * 10**6, bytes_accessed=us * 3 * 10**6, transcendentals=0)

    levels = [pltpu.VMEM((RING, count, LON), f32)] * (ADVECTION_TOTAL + 1)

    own = advective_ratio[0].reshape(ADVECTION_TOTAL * 2, count)
    held = -(-(count + LANES - math.gcd(count, LANES)) // LANES)
    own = lax.dynamic_update_slice(
        jnp.zeros((ADVECTION_TOTAL * 2, held * LANES), f32), own, (0, count * here % LANES)
    )
    own = jnp.transpose(own.reshape(ADVECTION_TOTAL * 2, held, LANES), (1, 0, 2))
    own = jnp.broadcast_to(own[None], (devices,) + own.shape)
    shared = lax.all_to_all(own, AXES, split_axis=0, concat_axis=0, tiled=True)

    states = jax.ShapeDtypeStruct((first * CELLS, LANES), f32)
    turned, state_of_cell = pl.pallas_call(
        turn_rows,
        out_shape=(states, jax.ShapeDtypeStruct((CELLS,), jnp.int32)),
        in_specs=[smem, hbm],
        out_specs=(hbm, smem),
        scratch_shapes=[pltpu.VMEM(covariance.shape, f32), pltpu.VMEM(states.shape, f32), sems, sems],
        compiler_params=params(60),
        cost_estimate=cost(10),
        name="turn_rows",
    )(cell_of_state, covariance)

    shape = (devices, block_rows(count), LANES)
    sent, rates = pl.pallas_call(
        first_pass,
        out_shape=(
            jax.ShapeDtypeStruct(shape, f32),
            jax.ShapeDtypeStruct((LAT + held, ADVECTION_TOTAL * 2, LON), f32),
        ),
        in_specs=[smem, smem, hbm, vmem, vmem],
        out_specs=(hbm, vmem),
        scratch_shapes=pass_scratch(first, count, shape) + [sems, sems] + levels,
        compiler_params=params(60),
        cost_estimate=cost(25),
        name="first_pass",
    )(cell_of_state, state_of_cell, turned, shared, flow_heading_flags)
    arrived = lax.all_to_all(sent, AXES, split_axis=0, concat_axis=0, tiled=True)

    lane = lax.broadcasted_iota(jnp.int32, (count, LANES), 1)
    row = lax.broadcasted_iota(jnp.int32, (count, LANES), 0)
    extra = jnp.where(lane == row % LANES, added_uncertainty[0][:, None], 0.0)
    return pl.pallas_call(
        second_pass,
        out_shape=jax.ShapeDtypeStruct((count, CELLS), f32),
        in_specs=[smem, smem, smem, hbm, vmem, vmem, vmem],
        out_specs=hbm,
        scratch_shapes=pass_scratch(second, LANES, (count, CELLS))
        + [sems, sems, pltpu.VMEM(shape, f32)]
        + levels,
        compiler_params=params(60),
        cost_estimate=cost(25),
        name="second_pass",
    )(cell_of_state, state_of_cell, here.reshape(1), arrived, rates, flow_heading_flags, extra)


def solution(mesh):
    in_specs = (
        P(AXES, None),
        P(None, None, None, AXES),
        P(),
        P(),
        P(None, AXES),
    )
    return jax.shard_map(shards, mesh=mesh, in_specs=in_specs, out_specs=P(AXES, None), check_vma=False)
```

time: 191 us -> 203 us (1.063)
  waiting for transfers between devices: 76 us -> 105 us
  Pallas kernels: 93.7 us -> 80.2 us
  starting transfers between devices: 16.8 us -> 13.5 us
    all_to_all x2 -> x1, waiting for transfers between devices: 76 us -> 105 us  [shards(): lax.all_to_all(sent, AXES, split_axis=0, concat_axis=0, tiled=True)]
    pallas_call x5 -> x3, Pallas kernels: 93.7 us -> 80.2 us  [the longest x1 34.9 us: shards(): pl.pallas_call(second_pass, out_shape=jax.ShapeDtypeStruct((count, CELLS)...]
    all_to_all x2 -> x1, starting transfers between devices: 9.5 us -> 6.13 us  [shards(): lax.all_to_all(sent, AXES, split_axis=0, concat_axis=0, tiled=True)]
  transfers between devices with their start and end apart: 3 -> 2, of which waited for: 2 -> 1; matrix products, arithmetic and copies ran while one was open for 1% -> 0% of each run, Pallas kernels for 24% -> 6%
where the time goes in v4:
time: 203 us; the launch traced here: 202 us
  waiting for transfers between devices  105 us (52%)
  Pallas kernels  80.2 us (40%)
  starting transfers between devices  13.5 us (7%)
  local copies, waits for them, and re-layouts  2.34 us (1%)
    all_to_all x1, waiting for transfers between devices, shards(): lax.all_to_all(sent, AXES, split_axis=0, concat_axis=0, tiled=True)  105 us
    pallas_call x1, Pallas kernels, shards(): pl.pallas_call(second_pass, out_shape=jax.ShapeDtypeStruct((count, CELLS)...  34.9 us
    pallas_call x1, Pallas kernels, shards(): pl.pallas_call(first_pass, out_shape=(jax.ShapeDtypeStruct(shape, f32), j...  34 us
    pallas_call x1, Pallas kernels, shards(): pl.pallas_call(turn_rows, out_shape=(states, jax.ShapeDtypeStruct((CELLS,...  11.4 us
    all_to_all x1, starting transfers between devices, shards(): shared = lax.all_to_all(own, AXES, split_axis=0, concat_axis=0, tiled=True)  7.33 us
    all_to_all x1, starting transfers between devices, shards(): lax.all_to_all(sent, AXES, split_axis=0, concat_axis=0, tiled=True)  6.13 us
  transfers between devices with their start and end apart: 2, of which 1 were waited for; matrix products, arithmetic and copies ran while one was open for 0% of the time, Pallas kernels for 6%

profile of v4, /device:TPU:0, one launch (start us, length us, event | category | flops | bytes accessed | tf_op | source)
XLA Modules:
  0.0 202.3 jit_solution(5957240275793744236)
XLA Ops:
  0.0 0.7 reshape_squeeze.3
  0.7 0.2 dynamic_update_slice.3
  0.9 0.7 broadcast_in_dim.24
  1.7 7.3 %all-to-all-start = ((f32[32,2,8,128]{3,2,1,0:T(8,128)}), f32[32,2,8,128]{3,2,1,0:T(8,128)S(1)}, u32[]{:S(2)}, u32[]{:S(2)}) async-start(f32[32,2,8,128]{3,2,1,0:T(8,128)} %broadcast_in_dim.24), calls=%async_computation | async-start | bytes 524288 | tf_op jit(solution)/shard_map/all_to_all | solution.py:332
  9.0 11.4 %turn_rows.1 = (f32[12288,128]{1,0:T(8,128)}, s32[6144]{0:T(1024)}) custom-call(s32[6144]{0:T(1024)} %cell_of_state.5, f32[192,6144]{1,0:T(8,128)} %x_hbm.1), custom_call_target="tpu_custom_call" | custom-call | flops 10000000 | bytes 30000000 | tf_op jit(solution)/shard_map/turn_rows/pallas_call | solution.py:335
  20.4 0.0 all-to-all-done.shared
  20.4 0.0 copy-start
  20.4 0.7 copy-done
  21.1 34.0 %first_pass.1 = (f32[32,288,128]{2,1,0:T(8,128)}, f32[50,8,128]{2,1,0:T(8,128)}) custom-call(s32[6144]{0:T(1024)} %cell_of_state.5, s32[6144]{0:T(1024)} %get-tuple-element.9.state_of_cell, f32[12288,128]{1,0:T(8,128)} %get-tuple-element.10.states_hbm, f32[32,2,8,128]{3,2,1,0:T(8,128)} %copy-done, s32[1,4,2,6144]{3,2,1,0:T(2,128)} %flags.3), custom_call_target="tpu_custom_call" | custom-call | flops 25000000 | bytes 75000000 | tf_op jit(solution)/shard_map/first_pass/pallas_call | solution.py:347
  55.1 0.0 copy-start.1
  55.1 6.1 %all-to-all-start.1 = ((f32[32,288,128]{2,1,0:T(8,128)}), f32[32,288,128]{2,1,0:T(8,128)}, u32[]{:S(2)}, u32[]{:S(2)}) async-start(f32[32,288,128]{2,1,0:T(8,128)} %get-tuple-element.11), calls=%async_computation.1 | async-start | bytes 9437184 | tf_op jit(solution)/shard_map/all_to_all | solution.py:360
  61.3 0.0 copy-done.1
  61.3 0.8 fusion.extra
  62.1 105.2 %all-to-all-done.1.a_hbm = f32[32,288,128]{2,1,0:T(8,128)} async-done(((f32[32,288,128]{2,1,0:T(8,128)}), f32[32,288,128]{2,1,0:T(8,128)}, u32[]{:S(2)}, u32[]{:S(2)}) %all-to-all-start.1) | async-done | bytes 4718624 | tf_op jit(solution)/shard_map/all_to_all | solution.py:360
  167.2 34.9 %second_pass.1 = f32[192,6144]{1,0:T(8,128)} custom-call(s32[6144]{0:T(1024)} %cell_of_state.5, s32[6144]{0:T(1024)} %get-tuple-element.9.state_of_cell, s32[1]{0:T(128)} %bitcast.place, f32[32,288,128]{2,1,0:T(8,128)} %all-to-all-done.1.a_hbm, f32[50,8,128]{2,1,0:T(8,128)} %get-tuple-element.12.rates, s32[1,4,2,6144]{3,2,1,0:T(2,128)} %flags.3, ...), custom_call_target="tpu_custom_call" | custom-call | flops 25000000 | bytes 75000000 | tf_op jit(solution)/shard_map/second_pass/pallas_call | solution.py:365
  (3 shorter events, 0.0 us)
Async XLA Ops:
  1.7 18.7 %all-to-all-start = ((f32[32,2,8,128]{3,2,1,0:T(8,128)}), f32[32,2,8,128]{3,2,1,0:T(8,128)S(1)}, u32[]{:S(2)}, u32[]{:S(2)}) async-start(f32[32,2,8,128]{3,2,1,0:T(8,128)} %broadcast_in_dim.24), calls=%async_computation | async-start | bytes 524288 | tf_op jit(solution)/shard_map/all_to_all | solution.py:332
  20.4 0.7 copy-start
  55.1 6.2 %copy-start.1 = (f32[1,192]{1,0:T(1,128)S(1)}, f32[1,192]{1,0:T(1,128)}, u32[]{:S(2)}) copy-start(f32[1,192]{1,0:T(1,128)} %param.9) | copy-start | bytes 2308
  55.1 112.2 %all-to-all-start.1 = ((f32[32,288,128]{2,1,0:T(8,128)}), f32[32,288,128]{2,1,0:T(8,128)}, u32[]{:S(2)}, u32[]{:S(2)}) async-start(f32[32,288,128]{2,1,0:T(8,128)} %get-tuple-element.11), calls=%async_computation.1 | async-start | bytes 9437184 | tf_op jit(solution)/shard_map/all_to_all | solution.py:360

commit v5 on v4

v5 whole, which is shorter than its diff:
```python
import math

import jax
import jax.numpy as jnp
from jax import lax
from jax.experimental import pallas as pl
from jax.experimental.pallas import tpu as pltpu
from jax.sharding import PartitionSpec as P

LAT = 48
LON = 128
ADVECTION_TOTAL = 4
CELLS = LAT * LON
LANES = 128
AXES = ("row", "col")
GROUPS = 4
BATCH = 16
BAND = 8
TURNS = 4
MIB = 2**20


def spans_first(count):
    half = count // 2
    return ((0, half), (half, half))


def spans_second(count):
    return tuple((at, min(LANES, count - at)) for at in range(0, count, LANES))


def is_packed(count, width):
    return 2 * width == LANES and count > width


def block_rows(count):
    return sum(count // 2 if is_packed(count, width) else count for _, width in spans_second(count))


def slot_rows(start, h, total, slots):
    return pl.ds(start + h, total, stride=slots) if slots > 1 else pl.ds(start, total)


def scatter_rows(index, start, source, target, slots, total):
    for u0 in range(0, total, BATCH):
        some = range(u0, min(u0 + BATCH, total))
        rows = [source[slots * u : slots * (u + 1), :] for u in some]
        for u, row in zip(some, rows):
            target[pl.ds(pl.multiple_of(slots * index[start + u], slots), slots), :] = row


def fill_and_place(fill, place, start, stop, last):
    def body(b, carry):
        i = 2 * b
        fill(i + 1, 1)
        place(i, 0)
        fill(jnp.minimum(i + 2, last), 0)
        place(i + 1, 1)
        return carry

    lax.fori_loop(start // 2, stop // 2, body, 0)


def substep(rates, flags, s, source, target, i):
    def spread(row):
        return jnp.broadcast_to(row, (8, LON))

    at_lane = pl.multiple_of(i * LON, LON)
    rate_x = rates[i, 2 * s : 2 * s + 1, :]
    rate_y = rates[i, 2 * s + 1 : 2 * s + 2, :]
    remain = spread(1.0 - rate_x - rate_y)
    lane = lax.broadcasted_iota(jnp.int32, (1, LON), 1)
    west = flags[0, s, 0:1, pl.ds(at_lane, LON)] == 1
    pick_x = spread(jnp.where(west, lane + (LON - 1), lane + 1) & (LON - 1))
    from_south = spread(flags[0, s, 1:2, pl.ds(at_lane, LON)]) == 1
    rate_x, rate_y = spread(rate_x), spread(rate_y)
    for g in range(0, source.shape[1], 8):
        here = source[i + 1, g : g + 8, :]
        side = jnp.take_along_axis(here, pick_x, axis=1)
        y_side = jnp.where(from_south, source[i, g : g + 8, :], source[i + 2, g : g + 8, :])
        target[i + 1, g : g + 8, :] = remain * here + rate_x * side + rate_y * y_side


def advect(spans, state_of_cell, rates, flags, packed, tiles, level_a, level_b):
    slots = len(spans)
    count = level_a.shape[1]

    def enter(b, carry):
        for i in range(TURNS):
            for h, (at, width) in enumerate(spans):
                block = packed[slot_rows(slots * LON * (TURNS * b + i), h, LON, slots), :]
                level_a[TURNS * b + i + 1, at : at + width, :] = block.T[:width]
        return carry

    lax.fori_loop(0, LAT // TURNS, enter, 0)
    for level in (level_a, level_b):
        for edge in (0, LAT + 1):
            level[edge] = jnp.zeros((count, LON), jnp.float32)
    source, target = level_a, level_b
    for s in range(ADVECTION_TOTAL):

        def band(b, carry, s=s, source=source, target=target):
            for i in range(BAND):
                substep(rates, flags, s, source, target, b * BAND + i)
            return carry

        lax.fori_loop(0, LAT // BAND, band, 0)
        source, target = target, source

    def leave(i, slot, final=source):
        for h, (at, width) in enumerate(spans):
            tiles[slot][slot_rows(0, h, LON, slots), 0:width] = final[i + 1, at : at + width, :].T

    def place(i, slot):
        scatter_rows(state_of_cell, i * LON, tiles[slot], packed, slots, LON)

    leave(0, 0)
    fill_and_place(leave, place, 0, LAT, LAT - 1)


def invert(cell_of_state, state_of_cell):
    unroll = 64

    def body(b, carry):
        for u in range(unroll):
            state_of_cell[cell_of_state[b * unroll + u]] = b * unroll + u
        return carry

    lax.fori_loop(0, CELLS // unroll, body, 0)


def gather_rates(shared, rates, count):
    rates[...] = jnp.zeros_like(rates)
    for d in range(shared.shape[0]):
        for t in range(shared.shape[1]):
            lat = d * count // LANES + t
            rates[lat] = rates[lat] + shared[d, t]


def first_pass(
    cell_of_state, state_of_cell, x_hbm, shared, flags, o_hbm, rates, x_v, packed, o_v, tile_a, tile_b, *rest
):
    (sem_in, sem_out), levels = rest[:2], rest[2:]
    tiles = (tile_a, tile_b)
    count = x_v.shape[0]
    devices = o_v.shape[0]
    spans = spans_first(count)
    slots = len(spans)
    half = count // 2
    wide = CELLS // GROUPS

    def fetch(q):
        part = pl.ds(q * wide, wide)
        return pltpu.make_async_copy(x_hbm.at[:, part], x_v.at[:, part], sem_in.at[q])

    for q in range(GROUPS):
        fetch(q).start()
    gather_rates(shared, rates, count)

    def turn(c, slot):
        at_lane = pl.multiple_of(c * LANES, LANES)
        for h, (at, width) in enumerate(spans):
            block = x_v[at : at + width, pl.ds(at_lane, LANES)]
            tiles[slot][slot_rows(0, h, LANES, slots), 0:width] = block.T

    def place(c, slot):
        scatter_rows(cell_of_state, c * LANES, tiles[slot], packed, slots, LANES)

    each = wide // LANES
    fetch(0).wait()
    turn(0, 0)
    for q in range(GROUPS):
        if q + 1 < GROUPS:
            fetch(q + 1).wait()
        fill_and_place(turn, place, q * each, (q + 1) * each, CELLS // LANES - 1)
    advect(spans, state_of_cell, rates, flags, packed, tiles, *levels)

    def pack(e):
        base = 0
        for at, width in spans_second(count):
            start = slots * (e * count + at)
            parts = [packed[slot_rows(start, h, width, slots), :] for h in range(slots)]
            if is_packed(count, width):
                o_v[e, base : base + half, :] = jnp.concatenate(parts, axis=0).T[:half]
                base += half
            else:
                for h in range(slots):
                    o_v[e, base : base + half, 0:width] = parts[h].T[:half]
                    base += half

    def pack_two(b, carry):
        pack(2 * b)
        pack(2 * b + 1)
        return carry

    some = devices // GROUPS

    def send(q):
        part = pl.ds(q * some, some)
        return pltpu.make_async_copy(o_v.at[part], o_hbm.at[part], sem_out.at[q])

    for q in range(GROUPS):
        lax.fori_loop(q * some // 2, (q + 1) * some // 2, pack_two, 0)
        send(q).start()
    for q in range(GROUPS):
        send(q).wait()


def second_pass(
    cell_of_state, state_of_cell, place, a_hbm, rates, flags, extra, o_hbm, a_v, packed, o_v, tile_a, tile_b, *rest
):
    (sem_in, sem_out), levels = rest[:2], rest[2:]
    tiles = (tile_a, tile_b)
    count = o_v.shape[0]
    devices = a_v.shape[0]
    spans = spans_second(count)
    slots = len(spans)
    half = count // 2
    some = devices // GROUPS

    def fetch(q):
        part = pl.ds(q * some, some)
        return pltpu.make_async_copy(a_hbm.at[part], a_v.at[part], sem_in.at[q])

    for q in range(GROUPS):
        fetch(q).start()

    def unpack(d, slot):
        tile = tiles[slot]
        base = 0
        for h, (_, width) in enumerate(spans):
            if is_packed(count, width):
                both = a_v[d, base : base + half, :]
                tile[slot_rows(0, h, half, slots), :] = both
                tile[slot_rows(slots * half, h, half, slots), :] = pltpu.roll(both, LANES // 2, 1)
                base += half
            else:
                tile[slot_rows(0, h, count, slots), :] = a_v[d, base : base + count, :]
                base += count

    def lay(d, slot):
        scatter_rows(cell_of_state, d * count, tiles[slot], packed, slots, count)

    fetch(0).wait()
    unpack(0, 0)
    for q in range(GROUPS):
        if q + 1 < GROUPS:
            fetch(q + 1).wait()
        fill_and_place(unpack, lay, q * some, (q + 1) * some, devices - 1)
    advect(spans, state_of_cell, rates, flags, packed, tiles, *levels)
    mine = pl.ds(pl.multiple_of(slots * count * place[0], 8), slots * count)
    packed[mine, :] = packed[mine, :] + extra[...]

    def turn(b, carry):
        for i in range(TURNS):
            c = TURNS * b + i
            at_lane = pl.multiple_of(c * LANES, LANES)
            for h, (at, width) in enumerate(spans):
                block = packed[slot_rows(slots * LANES * c, h, LANES, slots), :]
                o_v[at : at + width, pl.ds(at_lane, LANES)] = block.T[:width]
        return carry

    wide = CELLS // GROUPS

    def send(q):
        part = pl.ds(q * wide, wide)
        return pltpu.make_async_copy(o_v.at[:, part], o_hbm.at[:, part], sem_out.at[q])

    each = wide // LANES // TURNS
    for q in range(GROUPS):
        lax.fori_loop(q * each, (q + 1) * each, turn, 0)
        send(q).start()
    for q in range(GROUPS):
        send(q).wait()


def shards(covariance, advective_ratio, flow_heading_flags, cell_of_state, added_uncertainty):
    count = covariance.shape[0]
    devices = lax.axis_size(AXES)
    here = lax.axis_index(AXES)
    smem = pl.BlockSpec(memory_space=pltpu.SMEM)
    vmem = pl.BlockSpec(memory_space=pltpu.VMEM)
    hbm = pl.BlockSpec(memory_space=pl.ANY)
    f32 = jnp.float32
    first, second = len(spans_first(count)), len(spans_second(count))
    sems = pltpu.SemaphoreType.DMA((GROUPS,))

    def pass_scratch(slots, first_shape, last_shape):
        tile = pltpu.VMEM((slots * max(count, LANES), LANES), f32)
        level = pltpu.VMEM((LAT + 2, count, LON), f32)
        packed = pltpu.VMEM((slots * CELLS, LANES), f32)
        return [
            pltpu.VMEM(first_shape, f32),
            packed,
            pltpu.VMEM(last_shape, f32),
            tile,
            tile,
            sems,
            sems,
            level,
            level,
        ]

    def params(mib):
        return pltpu.CompilerParams(vmem_limit_bytes=mib * MIB)

    def cost(us):
        return pl.CostEstimate(flops=us * 10**6, bytes_accessed=us * 3 * 10**6, transcendentals=0)

    own = advective_ratio[0].reshape(ADVECTION_TOTAL * 2, count)
    held = -(-(count + LANES - math.gcd(count, LANES)) // LANES)
    own = lax.dynamic_update_slice(
        jnp.zeros((ADVECTION_TOTAL * 2, held * LANES), f32), own, (0, count * here % LANES)
    )
    own = jnp.transpose(own.reshape(ADVECTION_TOTAL * 2, held, LANES), (1, 0, 2))
    own = jnp.broadcast_to(own[None], (devices,) + own.shape)
    shared = lax.all_to_all(own, AXES, split_axis=0, concat_axis=0, tiled=True)

    state_of_cell = pl.pallas_call(
        invert,
        out_shape=jax.ShapeDtypeStruct((CELLS,), jnp.int32),
        in_specs=[smem],
        out_specs=smem,
        cost_estimate=cost(10),
        name="invert",
    )(cell_of_state)

    shape = (devices, block_rows(count), LANES)
    sent, rates = pl.pallas_call(
        first_pass,
        out_shape=(
            jax.ShapeDtypeStruct(shape, f32),
            jax.ShapeDtypeStruct((LAT + held, ADVECTION_TOTAL * 2, LON), f32),
        ),
        in_specs=[smem, smem, hbm, vmem, vmem],
        out_specs=(hbm, vmem),
        scratch_shapes=pass_scratch(first, covariance.shape, shape),
        compiler_params=params(60),
        cost_estimate=cost(25),
        name="first_pass",
    )(cell_of_state, state_of_cell, covariance, shared, flow_heading_flags)
    arrived = lax.all_to_all(sent, AXES, split_axis=0, concat_axis=0, tiled=True)

    row = lax.broadcasted_iota(jnp.int32, (count, second, LANES), 0)
    slot = lax.broadcasted_iota(jnp.int32, (count, second, LANES), 1) * LANES
    slot = slot + lax.broadcasted_iota(jnp.int32, (count, second, LANES), 2)
    extra = jnp.where(row == slot, added_uncertainty[0][:, None, None], 0.0).reshape(second * count, LANES)
    return pl.pallas_call(
        second_pass,
        out_shape=jax.ShapeDtypeStruct((count, CELLS), f32),
        in_specs=[smem, smem, smem, hbm, vmem, vmem, vmem],
        out_specs=hbm,
        scratch_shapes=pass_scratch(second, shape, (count, CELLS)),
        compiler_params=params(60),
        cost_estimate=cost(25),
        name="second_pass",
    )(cell_of_state, state_of_cell, here.reshape(1), arrived, rates, flow_heading_flags, extra)


def solution(mesh):
    in_specs = (
        P(AXES, None),
        P(None, None, None, AXES),
        P(),
        P(),
        P(None, AXES),
    )
    return jax.shard_map(shards, mesh=mesh, in_specs=in_specs, out_specs=P(AXES, None), check_vma=False)
```

time: 203 us -> 193 us (0.951)
  Pallas kernels: 80.2 us -> 70.8 us
    pallas_call x1, Pallas kernels: 34 us -> 30.5 us  [shards(): pl.pallas_call(first_pass, out_shape=(jax.ShapeDtypeStruct(shape, f32), j...]
    pallas_call x1, Pallas kernels: 34.9 us -> 31.5 us  [shards(): pl.pallas_call(second_pass, out_shape=jax.ShapeDtypeStruct((count, CELLS)...]
    pallas_call x1, Pallas kernels: 11.4 us -> 8.89 us  [shards(): pl.pallas_call(invert, out_shape=jax.ShapeDtypeStruct((CELLS,), jnp.int32...]
  transfers between devices with their start and end apart: 2 -> 2, of which waited for: 1 -> 2; matrix products, arithmetic and copies ran while one was open for 0% -> 1% of each run, Pallas kernels for 6% -> 5%
where the time goes in v5:
time: 193 us
  waiting for transfers between devices  106 us (55%)
  Pallas kernels  70.8 us (37%)
  starting transfers between devices  12.2 us (6%)
  local copies, waits for them, and re-layouts  2.87 us (1%)
    all_to_all x1, waiting for transfers between devices, shards(): lax.all_to_all(sent, AXES, split_axis=0, concat_axis=0, tiled=True)  105 us
    pallas_call x1, Pallas kernels, shards(): pl.pallas_call(second_pass, out_shape=jax.ShapeDtypeStruct((count, CELLS)...  31.5 us
    pallas_call x1, Pallas kernels, shards(): pl.pallas_call(first_pass, out_shape=(jax.ShapeDtypeStruct(shape, f32), j...  30.5 us
    pallas_call x1, Pallas kernels, shards(): pl.pallas_call(invert, out_shape=jax.ShapeDtypeStruct((CELLS,), jnp.int32...  8.89 us
    all_to_all x1, starting transfers between devices, shards(): shared = lax.all_to_all(own, AXES, split_axis=0, concat_axis=0, tiled=True)  7.33 us
    all_to_all x1, starting transfers between devices, shards(): lax.all_to_all(sent, AXES, split_axis=0, concat_axis=0, tiled=True)  4.86 us
  transfers between devices with their start and end apart: 2, of which 2 were waited for; matrix products, arithmetic and copies ran while one was open for 1% of the time, Pallas kernels for 5%

profile of v5, /device:TPU:0, one launch (start us, length us, event | category | flops | bytes accessed | tf_op | source)
XLA Modules:
  0.0 192.7 jit_solution(284760443501211516)
XLA Ops:
  0.0 0.7 reshape_squeeze.3
  0.7 0.2 dynamic_update_slice.3
  0.9 0.7 broadcast_in_dim.28
  1.7 7.3 %all-to-all-start = ((f32[32,2,8,128]{3,2,1,0:T(8,128)}), f32[32,2,8,128]{3,2,1,0:T(8,128)S(1)}, u32[]{:S(2)}, u32[]{:S(2)}) async-start(f32[32,2,8,128]{3,2,1,0:T(8,128)} %broadcast_in_dim.28), calls=%async_computation | async-start | bytes 524288 | tf_op jit(solution)/shard_map/all_to_all | solution.py:317
  9.0 8.9 %invert.1.state_of_cell = s32[6144]{0:T(1024)} custom-call(s32[6144]{0:T(1024)} %cell_of_state.5), custom_call_target="tpu_custom_call" | custom-call | flops 10000000 | bytes 30000000 | tf_op jit(solution)/shard_map/invert/pallas_call | solution.py:319
  17.9 1.1 all-to-all-done.shared
  19.0 0.0 copy-start
  19.0 0.7 copy-done
  19.7 30.5 %first_pass.1 = (f32[32,288,128]{2,1,0:T(8,128)}, f32[50,8,128]{2,1,0:T(8,128)}) custom-call(s32[6144]{0:T(1024)} %cell_of_state.5, s32[6144]{0:T(1024)} %invert.1.state_of_cell, f32[192,6144]{1,0:T(8,128)} %x_hbm.1, f32[32,2,8,128]{3,2,1,0:T(8,128)} %copy-done, s32[1,4,2,6144]{3,2,1,0:T(2,128)} %flags.3), custom_call_target="tpu_custom_call" | custom-call | flops 25000000 | bytes 75000000 | tf_op jit(solution)/shard_map/first_pass/pallas_call | solution.py:329
  50.2 0.0 copy-start.1
  50.2 4.9 %all-to-all-start.1 = ((f32[32,288,128]{2,1,0:T(8,128)}), f32[32,288,128]{2,1,0:T(8,128)}, u32[]{:S(2)}, u32[]{:S(2)}) async-start(f32[32,288,128]{2,1,0:T(8,128)} %get-tuple-element.7), calls=%async_computation.1 | async-start | bytes 9437184 | tf_op jit(solution)/shard_map/all_to_all | solution.py:342
  55.1 0.1 iota.32
  55.2 0.0 copy-done.1
  55.2 0.1 broadcast_in_dim.30
  55.3 0.1 broadcast_in_dim.31
  55.5 0.1 iota.28
  55.6 0.9 fusion.extra
  56.5 104.7 %all-to-all-done.1.a_hbm = f32[32,288,128]{2,1,0:T(8,128)} async-done(((f32[32,288,128]{2,1,0:T(8,128)}), f32[32,288,128]{2,1,0:T(8,128)}, u32[]{:S(2)}, u32[]{:S(2)}) %all-to-all-start.1) | async-done | bytes 4718624 | tf_op jit(solution)/shard_map/all_to_all | solution.py:342
  161.3 31.5 %second_pass.1 = f32[192,6144]{1,0:T(8,128)} custom-call(s32[6144]{0:T(1024)} %cell_of_state.5, s32[6144]{0:T(1024)} %invert.1.state_of_cell, s32[1]{0:T(128)} %bitcast.place, f32[32,288,128]{2,1,0:T(8,128)} %all-to-all-done.1.a_hbm, f32[50,8,128]{2,1,0:T(8,128)} %get-tuple-element.8.rates, s32[1,4,2,6144]{3,2,1,0:T(2,128)} %flags.3, f32[384,128]{1,0:T(8,128)} %fusion.extra), custom_call_target="tpu_custom_call" | custom-call | flops 25000000 | bytes 75000000 | tf_op jit(solution)/shard_map/second_pass/pallas_call | solution.py:348
  (4 shorter events, 0.0 us)
Async XLA Ops:
  1.7 17.3 %all-to-all-start = ((f32[32,2,8,128]{3,2,1,0:T(8,128)}), f32[32,2,8,128]{3,2,1,0:T(8,128)S(1)}, u32[]{:S(2)}, u32[]{:S(2)}) async-start(f32[32,2,8,128]{3,2,1,0:T(8,128)} %broadcast_in_dim.28), calls=%async_computation | async-start | bytes 524288 | tf_op jit(solution)/shard_map/all_to_all | solution.py:317
  19.0 0.7 copy-start
  50.2 5.1 %copy-start.1 = (f32[1,192]{1,0:T(1,128)S(1)}, f32[1,192]{1,0:T(1,128)}, u32[]{:S(2)}) copy-start(f32[1,192]{1,0:T(1,128)} %param.9) | copy-start | bytes 2308
  50.2 111.1 %all-to-all-start.1 = ((f32[32,288,128]{2,1,0:T(8,128)}), f32[32,288,128]{2,1,0:T(8,128)}, u32[]{:S(2)}, u32[]{:S(2)}) async-start(f32[32,288,128]{2,1,0:T(8,128)} %get-tuple-element.7), calls=%async_computation.1 | async-start | bytes 9437184 | tf_op jit(solution)/shard_map/all_to_all | solution.py:342

commit v6 on v5

--- a/solution.py
+++ b/solution.py
@@ -13,10 +13,10 @@
 CELLS = LAT * LON
 LANES = 128
 AXES = ("row", "col")
-GROUPS = 4
+GROUPS = 8
 BATCH = 16
-BAND = 8
-TURNS = 4
+BAND = 16
+TURNS = 6
 MIB = 2**20
 
 
@@ -46,7 +46,7 @@
         some = range(u0, min(u0 + BATCH, total))
         rows = [source[slots * u : slots * (u + 1), :] for u in some]
         for u, row in zip(some, rows):
-            target[pl.ds(pl.multiple_of(slots * index[start + u], slots), slots), :] = row
+            target[pl.ds(pl.multiple_of(index[start + u], slots), slots), :] = row
 
 
 def fill_and_place(fill, place, start, stop, last):
@@ -118,15 +118,18 @@
     fill_and_place(leave, place, 0, LAT, LAT - 1)
 
 
-def invert(cell_of_state, state_of_cell):
+def invert(slots):
     unroll = 64
 
-    def body(b, carry):
-        for u in range(unroll):
-            state_of_cell[cell_of_state[b * unroll + u]] = b * unroll + u
-        return carry
-
-    lax.fori_loop(0, CELLS // unroll, body, 0)
+    def kernel(cell_of_state, state_of_cell):
+        def body(b, carry):
+            for u in range(unroll):
+                state_of_cell[cell_of_state[b * unroll + u]] = slots * (b * unroll + u)
+            return carry
+
+        lax.fori_loop(0, CELLS // unroll, body, 0)
+
+    return kernel
 
 
 def gather_rates(shared, rates, count):
@@ -316,8 +319,9 @@
     own = jnp.broadcast_to(own[None], (devices,) + own.shape)
     shared = lax.all_to_all(own, AXES, split_axis=0, concat_axis=0, tiled=True)
 
-    state_of_cell = pl.pallas_call(
-        invert,
+    cells_first = first * cell_of_state
+    states_first = pl.pallas_call(
+        invert(first),
         out_shape=jax.ShapeDtypeStruct((CELLS,), jnp.int32),
         in_specs=[smem],
         out_specs=smem,
@@ -338,13 +342,16 @@
         compiler_params=params(60),
         cost_estimate=cost(25),
         name="first_pass",
-    )(cell_of_state, state_of_cell, covariance, shared, flow_heading_flags)
+    )(cells_first, states_first, covariance, shared, flow_heading_flags)
     arrived = lax.all_to_all(sent, AXES, split_axis=0, concat_axis=0, tiled=True)
 
     row = lax.broadcasted_iota(jnp.int32, (count, second, LANES), 0)
     slot = lax.broadcasted_iota(jnp.int32, (count, second, LANES), 1) * LANES
     slot = slot + lax.broadcasted_iota(jnp.int32, (count, second, LANES), 2)
     extra = jnp.where(row == slot, added_uncertainty[0][:, None, None], 0.0).reshape(second * count, LANES)
+    cells_second, states_second = cells_first, states_first
+    if first != second:
+        cells_second, states_second = second * cell_of_state, states_first // first * second
     return pl.pallas_call(
         second_pass,
         out_shape=jax.ShapeDtypeStruct((count, CELLS), f32),
@@ -354,7 +361,7 @@
         compiler_params=params(60),
         cost_estimate=cost(25),
         name="second_pass",
-    )(cell_of_state, state_of_cell, here.reshape(1), arrived, rates, flow_heading_flags, extra)
+    )(cells_second, states_second, here.reshape(1), arrived, rates, flow_heading_flags, extra)
 
 
 def solution(mesh):

time: 193 us -> 185 us (0.959)
  Pallas kernels: 70.8 us -> 61.4 us
    pallas_call x1, Pallas kernels: 31.5 us -> 25.4 us  [shards(): pl.pallas_call(second_pass, out_shape=jax.ShapeDtypeStruct((count, CELLS)...]
    pallas_call x1, Pallas kernels: 30.5 us -> 25.5 us  [shards(): pl.pallas_call(first_pass, out_shape=(jax.ShapeDtypeStruct(shape, f32), j...]
  transfers between devices with their start and end apart: 2 -> 2, of which waited for: 2 -> 1; matrix products, arithmetic and copies ran while one was open for 1% -> 2% of each run, Pallas kernels for 5% -> 6%
where the time goes in v6:
time: 185 us
  waiting for transfers between devices  105 us (57%)
  Pallas kernels  61.4 us (33%)
  starting transfers between devices  13.5 us (7%)
  local copies, waits for them, and re-layouts  2.87 us (2%)
  other arithmetic  2.26 us (1%)
    all_to_all x1, waiting for transfers between devices, shards(): lax.all_to_all(sent, AXES, split_axis=0, concat_axis=0, tiled=True)  105 us
    pallas_call x1, Pallas kernels, shards(): pl.pallas_call(first_pass, out_shape=(jax.ShapeDtypeStruct(shape, f32), j...  25.5 us
    pallas_call x1, Pallas kernels, shards(): pl.pallas_call(second_pass, out_shape=jax.ShapeDtypeStruct((count, CELLS)...  25.4 us
    pallas_call x1, Pallas kernels, shards(): pl.pallas_call(invert(first), out_shape=jax.ShapeDtypeStruct((CELLS,), jn...  10.5 us
    all_to_all x1, starting transfers between devices, shards(): shared = lax.all_to_all(own, AXES, split_axis=0, concat_axis=0, tiled=True)  7.33 us
    all_to_all x1, starting transfers between devices, shards(): lax.all_to_all(sent, AXES, split_axis=0, concat_axis=0, tiled=True)  6.13 us
  transfers between devices with their start and end apart: 2, of which 1 were waited for; matrix products, arithmetic and copies ran while one was open for 2% of the time, Pallas kernels for 6%

profile of v6, /device:TPU:0, one launch (start us, length us, event | category | flops | bytes accessed | tf_op | source)
XLA Modules:
  0.0 184.8 jit_solution(18024165525714336129)
XLA Ops:
  0.0 0.7 reshape_squeeze.3
  0.7 0.2 dynamic_update_slice.3
  0.9 0.7 broadcast_in_dim.28
  1.7 7.3 %all-to-all-start = ((f32[32,2,8,128]{3,2,1,0:T(8,128)}), f32[32,2,8,128]{3,2,1,0:T(8,128)S(1)}, u32[]{:S(2)}, u32[]{:S(2)}) async-start(f32[32,2,8,128]{3,2,1,0:T(8,128)} %broadcast_in_dim.28), calls=%async_computation | async-start | bytes 524288 | tf_op jit(solution)/shard_map/all_to_all | solution.py:320
  9.0 10.5 %invert.1.state_of_cell = s32[6144]{0:T(1024)} custom-call(s32[6144]{0:T(1024)} %cell_of_state.1), custom_call_target="tpu_custom_call" | custom-call | flops 10000000 | bytes 30000000 | tf_op jit(solution)/shard_map/invert/pallas_call | solution.py:323
  19.5 1.3 broadcast_multiply_fusion.cell_of_state
  20.8 0.0 all-to-all-done.shared
  20.9 0.0 copy-start
  20.9 0.7 copy-done
  21.6 25.5 %first_pass.1 = (f32[32,288,128]{2,1,0:T(8,128)}, f32[50,8,128]{2,1,0:T(8,128)}) custom-call(s32[6144]{0:T(1024)} %broadcast_multiply_fusion.cell_of_state, s32[6144]{0:T(1024)} %invert.1.state_of_cell, f32[192,6144]{1,0:T(8,128)} %x_hbm.1, f32[32,2,8,128]{3,2,1,0:T(8,128)} %copy-done, s32[1,4,2,6144]{3,2,1,0:T(2,128)} %flags.3), custom_call_target="tpu_custom_call" | custom-call | flops 25000000 | bytes 75000000 | tf_op jit(solution)/shard_map/first_pass/pallas_call | solution.py:333
  47.1 0.0 copy-start.1
  47.1 6.1 %all-to-all-start.1 = ((f32[32,288,128]{2,1,0:T(8,128)}), f32[32,288,128]{2,1,0:T(8,128)}, u32[]{:S(2)}, u32[]{:S(2)}) async-start(f32[32,288,128]{2,1,0:T(8,128)} %get-tuple-element.7), calls=%async_computation.1 | async-start | bytes 9437184 | tf_op jit(solution)/shard_map/all_to_all | solution.py:346
  53.3 0.1 iota.32
  53.4 0.0 copy-done.1
  53.4 0.1 broadcast_in_dim.30
  53.5 0.1 broadcast_in_dim.31
  53.7 0.1 iota.28
  53.8 0.9 fusion.extra
  54.7 104.5 %all-to-all-done.1.a_hbm = f32[32,288,128]{2,1,0:T(8,128)} async-done(((f32[32,288,128]{2,1,0:T(8,128)}), f32[32,288,128]{2,1,0:T(8,128)}, u32[]{:S(2)}, u32[]{:S(2)}) %all-to-all-start.1) | async-done | bytes 4718624 | tf_op jit(solution)/shard_map/all_to_all | solution.py:346
  159.3 25.4 %second_pass.1 = f32[192,6144]{1,0:T(8,128)} custom-call(s32[6144]{0:T(1024)} %broadcast_multiply_fusion.cell_of_state, s32[6144]{0:T(1024)} %invert.1.state_of_cell, s32[1]{0:T(128)} %bitcast.place, f32[32,288,128]{2,1,0:T(8,128)} %all-to-all-done.1.a_hbm, f32[50,8,128]{2,1,0:T(8,128)} %get-tuple-element.8.rates, s32[1,4,2,6144]{3,2,1,0:T(2,128)} %flags.3, ...), custom_call_target="tpu_custom_call" | custom-call | flops 25000000 | bytes 75000000 | tf_op jit(solution)/shard_map/second_pass/pallas_call | solution.py:355
  (4 shorter events, 0.0 us)
Async XLA Ops:
  1.7 19.2 %all-to-all-start = ((f32[32,2,8,128]{3,2,1,0:T(8,128)}), f32[32,2,8,128]{3,2,1,0:T(8,128)S(1)}, u32[]{:S(2)}, u32[]{:S(2)}) async-start(f32[32,2,8,128]{3,2,1,0:T(8,128)} %broadcast_in_dim.28), calls=%async_computation | async-start | bytes 524288 | tf_op jit(solution)/shard_map/all_to_all | solution.py:320
  20.9 0.7 copy-start
  47.1 6.3 %copy-start.1 = (f32[1,192]{1,0:T(1,128)S(1)}, f32[1,192]{1,0:T(1,128)}, u32[]{:S(2)}) copy-start(f32[1,192]{1,0:T(1,128)} %param.9) | copy-start | bytes 2308
  47.1 112.2 %all-to-all-start.1 = ((f32[32,288,128]{2,1,0:T(8,128)}), f32[32,288,128]{2,1,0:T(8,128)}, u32[]{:S(2)}, u32[]{:S(2)}) async-start(f32[32,288,128]{2,1,0:T(8,128)} %get-tuple-element.7), calls=%async_computation.1 | async-start | bytes 9437184 | tf_op jit(solution)/shard_map/all_to_all | solution.py:346

commit v7 on v6

--- a/solution.py
+++ b/solution.py
@@ -81,7 +81,7 @@
         target[i + 1, g : g + 8, :] = remain * here + rate_x * side + rate_y * y_side
 
 
-def advect(spans, state_of_cell, rates, flags, packed, tiles, level_a, level_b):
+def advect(spans, state_of_cell, rates, flags, packed, tiles, level_a, level_b, aside=None):
     slots = len(spans)
     count = level_a.shape[1]
 
@@ -102,6 +102,8 @@
         def band(b, carry, s=s, source=source, target=target):
             for i in range(BAND):
                 substep(rates, flags, s, source, target, b * BAND + i)
+            if aside is not None:
+                aside(b + s * (LAT // BAND))
             return carry
 
         lax.fori_loop(0, LAT // BAND, band, 0)
@@ -116,20 +118,6 @@
 
     leave(0, 0)
     fill_and_place(leave, place, 0, LAT, LAT - 1)
-
-
-def invert(slots):
-    unroll = 64
-
-    def kernel(cell_of_state, state_of_cell):
-        def body(b, carry):
-            for u in range(unroll):
-                state_of_cell[cell_of_state[b * unroll + u]] = slots * (b * unroll + u)
-            return carry
-
-        lax.fori_loop(0, CELLS // unroll, body, 0)
-
-    return kernel
 
 
 def gather_rates(shared, rates, count):
@@ -141,7 +129,7 @@
 
 
 def first_pass(
-    cell_of_state, state_of_cell, x_hbm, shared, flags, o_hbm, rates, x_v, packed, o_v, tile_a, tile_b, *rest
+    cell_of_state, cells, x_hbm, shared, flags, o_hbm, rates, state_of_cell, x_v, packed, o_v, tile_a, tile_b, *rest
 ):
     (sem_in, sem_out), levels = rest[:2], rest[2:]
     tiles = (tile_a, tile_b)
@@ -176,7 +164,14 @@
         if q + 1 < GROUPS:
             fetch(q + 1).wait()
         fill_and_place(turn, place, q * each, (q + 1) * each, CELLS // LANES - 1)
-    advect(spans, state_of_cell, rates, flags, packed, tiles, *levels)
+
+    def invert(n):
+        share = CELLS * BAND // (LAT * ADVECTION_TOTAL)
+        base, value = n * share, n * (slots * share)
+        for u in range(share):
+            state_of_cell[cells[base + u]] = value + slots * u
+
+    advect(spans, state_of_cell, rates, flags, packed, tiles, *levels, aside=invert)
 
     def pack(e):
         base = 0
@@ -320,29 +315,21 @@
     shared = lax.all_to_all(own, AXES, split_axis=0, concat_axis=0, tiled=True)
 
     cells_first = first * cell_of_state
-    states_first = pl.pallas_call(
-        invert(first),
-        out_shape=jax.ShapeDtypeStruct((CELLS,), jnp.int32),
-        in_specs=[smem],
-        out_specs=smem,
-        cost_estimate=cost(10),
-        name="invert",
-    )(cell_of_state)
-
     shape = (devices, block_rows(count), LANES)
-    sent, rates = pl.pallas_call(
+    sent, rates, states_first = pl.pallas_call(
         first_pass,
         out_shape=(
             jax.ShapeDtypeStruct(shape, f32),
             jax.ShapeDtypeStruct((LAT + held, ADVECTION_TOTAL * 2, LON), f32),
+            jax.ShapeDtypeStruct((CELLS,), jnp.int32),
         ),
         in_specs=[smem, smem, hbm, vmem, vmem],
-        out_specs=(hbm, vmem),
+        out_specs=(hbm, vmem, smem),
         scratch_shapes=pass_scratch(first, covariance.shape, shape),
         compiler_params=params(60),
         cost_estimate=cost(25),
         name="first_pass",
-    )(cells_first, states_first, covariance, shared, flow_heading_flags)
+    )(cells_first, cell_of_state, covariance, shared, flow_heading_flags)
     arrived = lax.all_to_all(sent, AXES, split_axis=0, concat_axis=0, tiled=True)
 
     row = lax.broadcasted_iota(jnp.int32, (count, second, LANES), 0)

time: 185 us -> 185 us (level)
  waiting for transfers between devices: 105 us -> 113 us
  Pallas kernels: 61.4 us -> 55.1 us
  starting transfers between devices: 13.5 us -> 11.1 us
    pallas_call x1 -> x0, Pallas kernels: 10.5 us -> none  [shards(): pl.pallas_call(invert(first), out_shape=jax.ShapeDtypeStruct((CELLS,), jn...]
    all_to_all x1, waiting for transfers between devices: 0.01 us -> 8.66 us  [shards(): shared = lax.all_to_all(own, AXES, split_axis=0, concat_axis=0, tiled=True)]
    pallas_call x1, Pallas kernels: 25.5 us -> 29.7 us  [shards(): pl.pallas_call(first_pass, out_shape=(jax.ShapeDtypeStruct(shape, f32), j...]
    all_to_all x1, starting transfers between devices: 6.13 us -> 3.78 us  [shards(): lax.all_to_all(sent, AXES, split_axis=0, concat_axis=0, tiled=True)]
  transfers between devices with their start and end apart: 2 -> 2, of which waited for: 1 -> 2; matrix products, arithmetic and copies ran while one was open for 2% -> 2% of each run, Pallas kernels for 6% -> 0%
where the time goes in v7:
time: 185 us
  waiting for transfers between devices  113 us (61%)
  Pallas kernels  55.1 us (30%)
  starting transfers between devices  11.1 us (6%)
  local copies, waits for them, and re-layouts  2.87 us (2%)
  other arithmetic  2.26 us (1%)
    all_to_all x1, waiting for transfers between devices, shards(): lax.all_to_all(sent, AXES, split_axis=0, concat_axis=0, tiled=True)  105 us
    pallas_call x1, Pallas kernels, shards(): pl.pallas_call(first_pass, out_shape=(jax.ShapeDtypeStruct(shape, f32), j...  29.7 us
    pallas_call x1, Pallas kernels, shards(): pl.pallas_call(second_pass, out_shape=jax.ShapeDtypeStruct((count, CELLS)...  25.4 us
    all_to_all x1, waiting for transfers between devices, shards(): shared = lax.all_to_all(own, AXES, split_axis=0, concat_axis=0, tiled=True)  8.66 us
    all_to_all x1, starting transfers between devices, shards(): shared = lax.all_to_all(own, AXES, split_axis=0, concat_axis=0, tiled=True)  7.33 us
    all_to_all x1, starting transfers between devices, shards(): lax.all_to_all(sent, AXES, split_axis=0, concat_axis=0, tiled=True)  3.78 us
  transfers between devices with their start and end apart: 2, of which 2 were waited for; matrix products, arithmetic and copies ran while one was open for 2% of the time, Pallas kernels for 0%

profile of v7, /device:TPU:0, one launch (start us, length us, event | category | flops | bytes accessed | tf_op | source)
XLA Modules:
  0.0 184.8 jit_solution(147936520552177352)
XLA Ops:
  0.0 0.7 reshape_squeeze.3
  0.7 0.2 dynamic_update_slice.3
  0.9 0.7 broadcast_in_dim.28
  1.7 7.3 %all-to-all-start = ((f32[32,2,8,128]{3,2,1,0:T(8,128)}), f32[32,2,8,128]{3,2,1,0:T(8,128)S(1)}, u32[]{:S(2)}, u32[]{:S(2)}) async-start(f32[32,2,8,128]{3,2,1,0:T(8,128)} %broadcast_in_dim.28), calls=%async_computation | async-start | bytes 524288 | tf_op jit(solution)/shard_map/all_to_all | solution.py:315
  9.0 1.3 broadcast_multiply_fusion.cell_of_state
  10.3 8.7 %all-to-all-done.shared = f32[32,2,8,128]{3,2,1,0:T(8,128)S(1)} async-done(((f32[32,2,8,128]{3,2,1,0:T(8,128)}), f32[32,2,8,128]{3,2,1,0:T(8,128)S(1)}, u32[]{:S(2)}, u32[]{:S(2)}) %all-to-all-start) | async-done | bytes 262176 | tf_op jit(solution)/shard_map/all_to_all | solution.py:315
  19.0 0.0 copy-start
  19.0 0.7 copy-done
  19.7 29.7 %first_pass.1 = (f32[32,288,128]{2,1,0:T(8,128)}, f32[50,8,128]{2,1,0:T(8,128)}, s32[6144]{0:T(1024)}) custom-call(s32[6144]{0:T(1024)} %broadcast_multiply_fusion.cell_of_state, s32[6144]{0:T(1024)} %cells.1, f32[192,6144]{1,0:T(8,128)} %x_hbm.1, f32[32,2,8,128]{3,2,1,0:T(8,128)} %copy-done, s32[1,4,2,6144]{3,2,1,0:T(2,128)} %flags.3), custom_call_target="tpu_custom_call" | custom-call | flops 25000000 | bytes 75000000 | tf_op jit(solution)/shard_map/first_pass/pallas_call | solution.py:319
  49.4 0.0 copy-start.1
  49.4 3.8 %all-to-all-start.1 = ((f32[32,288,128]{2,1,0:T(8,128)}), f32[32,288,128]{2,1,0:T(8,128)}, u32[]{:S(2)}, u32[]{:S(2)}) async-start(f32[32,288,128]{2,1,0:T(8,128)} %get-tuple-element.9), calls=%async_computation.1 | async-start | bytes 9437184 | tf_op jit(solution)/shard_map/all_to_all | solution.py:333
  53.3 0.1 iota.32
  53.4 0.0 copy-done.1
  53.4 0.1 broadcast_in_dim.30
  53.5 0.1 broadcast_in_dim.31
  53.7 0.1 iota.28
  53.8 0.9 fusion.extra
  54.7 104.5 %all-to-all-done.1.a_hbm = f32[32,288,128]{2,1,0:T(8,128)} async-done(((f32[32,288,128]{2,1,0:T(8,128)}), f32[32,288,128]{2,1,0:T(8,128)}, u32[]{:S(2)}, u32[]{:S(2)}) %all-to-all-start.1) | async-done | bytes 4718624 | tf_op jit(solution)/shard_map/all_to_all | solution.py:333
  159.2 25.4 %second_pass.1 = f32[192,6144]{1,0:T(8,128)} custom-call(s32[6144]{0:T(1024)} %broadcast_multiply_fusion.cell_of_state, s32[6144]{0:T(1024)} %get-tuple-element.8.state_of_cell, s32[1]{0:T(128)} %bitcast.2.place, f32[32,288,128]{2,1,0:T(8,128)} %all-to-all-done.1.a_hbm, f32[50,8,128]{2,1,0:T(8,128)} %get-tuple-element.10.rates, s32[1,4,2,6144]{3,2,1,0:T(2,128)} %flags.3, ...), custom_call_target="tpu_custom_call" | custom-call | flops 25000000 | bytes 75000000 | tf_op jit(solution)/shard_map/second_pass/pallas_call | solution.py:342
  (4 shorter events, 0.0 us)
Async XLA Ops:
  1.7 17.3 %all-to-all-start = ((f32[32,2,8,128]{3,2,1,0:T(8,128)}), f32[32,2,8,128]{3,2,1,0:T(8,128)S(1)}, u32[]{:S(2)}, u32[]{:S(2)}) async-start(f32[32,2,8,128]{3,2,1,0:T(8,128)} %broadcast_in_dim.28), calls=%async_computation | async-start | bytes 524288 | tf_op jit(solution)/shard_map/all_to_all | solution.py:315
  19.0 0.7 copy-start
  49.4 4.0 %copy-start.1 = (f32[1,192]{1,0:T(1,128)S(1)}, f32[1,192]{1,0:T(1,128)}, u32[]{:S(2)}) copy-start(f32[1,192]{1,0:T(1,128)} %param.9) | copy-start | bytes 2308
  49.4 109.8 %all-to-all-start.1 = ((f32[32,288,128]{2,1,0:T(8,128)}), f32[32,288,128]{2,1,0:T(8,128)}, u32[]{:S(2)}, u32[]{:S(2)}) async-start(f32[32,288,128]{2,1,0:T(8,128)} %get-tuple-element.9), calls=%async_computation.1 | async-start | bytes 9437184 | tf_op jit(solution)/shard_map/all_to_all | solution.py:333

commit v8 on v6

--- a/solution.py
+++ b/solution.py
@@ -119,12 +119,15 @@
 
 
 def invert(slots):
-    unroll = 64
-
-    def kernel(cell_of_state, state_of_cell):
+    unroll = 128
+
+    def kernel(cell_of_state, cells, state_of_cell, scaled):
+        scaled[...] = slots * cells[...]
+
         def body(b, carry):
+            base, value = b * unroll, b * (slots * unroll)
             for u in range(unroll):
-                state_of_cell[cell_of_state[b * unroll + u]] = slots * (b * unroll + u)
+                state_of_cell[cell_of_state[base + u]] = value + slots * u
             return carry
 
         lax.fori_loop(0, CELLS // unroll, body, 0)
@@ -319,15 +322,18 @@
     own = jnp.broadcast_to(own[None], (devices,) + own.shape)
     shared = lax.all_to_all(own, AXES, split_axis=0, concat_axis=0, tiled=True)
 
-    cells_first = first * cell_of_state
-    states_first = pl.pallas_call(
+    states_first, cells_first = pl.pallas_call(
         invert(first),
-        out_shape=jax.ShapeDtypeStruct((CELLS,), jnp.int32),
-        in_specs=[smem],
-        out_specs=smem,
+        out_shape=(
+            jax.ShapeDtypeStruct((CELLS,), jnp.int32),
+            jax.ShapeDtypeStruct((LAT, LON), jnp.int32),
+        ),
+        in_specs=[smem, vmem],
+        out_specs=(smem, vmem),
         cost_estimate=cost(10),
         name="invert",
-    )(cell_of_state)
+    )(cell_of_state, cell_of_state.reshape(LAT, LON))
+    cells_first = cells_first.reshape(CELLS)
 
     shape = (devices, block_rows(count), LANES)
     sent, rates = pl.pallas_call(

time: 185 us -> 184 us (level)
  transfers between devices with their start and end apart: 2 -> 2, of which waited for: 1 -> 1; matrix products, arithmetic and copies ran while one was open for 2% -> 1% of each run, Pallas kernels for 6% -> 6%
where the time goes in v8:
time: 184 us; the launch traced here: 183 us
  waiting for transfers between devices  105 us (57%)
  Pallas kernels  61.2 us (33%)
  starting transfers between devices  13.5 us (7%)
  local copies, waits for them, and re-layouts  2.86 us (2%)
    all_to_all x1, waiting for transfers between devices, shards(): lax.all_to_all(sent, AXES, split_axis=0, concat_axis=0, tiled=True)  105 us
    pallas_call x1, Pallas kernels, shards(): pl.pallas_call(first_pass, out_shape=(jax.ShapeDtypeStruct(shape, f32), j...  25.6 us
    pallas_call x1, Pallas kernels, shards(): pl.pallas_call(second_pass, out_shape=jax.ShapeDtypeStruct((count, CELLS)...  25.4 us
    pallas_call x1, Pallas kernels, shards(): pl.pallas_call(invert(first), out_shape=(jax.ShapeDtypeStruct((CELLS,), j...  10.3 us
    all_to_all x1, starting transfers between devices, shards(): shared = lax.all_to_all(own, AXES, split_axis=0, concat_axis=0, tiled=True)  7.33 us
    all_to_all x1, starting transfers between devices, shards(): lax.all_to_all(sent, AXES, split_axis=0, concat_axis=0, tiled=True)  6.13 us
  transfers between devices with their start and end apart: 2, of which 1 were waited for; matrix products, arithmetic and copies ran while one was open for 1% of the time, Pallas kernels for 6%

profile of v8, /device:TPU:0, one launch (start us, length us, event | category | flops | bytes accessed | tf_op | source)
XLA Modules:
  0.0 183.2 jit_solution(10950989839063065559)
XLA Ops:
  0.0 0.7 reshape_squeeze.3
  0.7 0.2 dynamic_update_slice.3
  0.9 0.7 broadcast_in_dim.28
  1.7 7.3 %all-to-all-start = ((f32[32,2,8,128]{3,2,1,0:T(8,128)}), f32[32,2,8,128]{3,2,1,0:T(8,128)S(1)}, u32[]{:S(2)}, u32[]{:S(2)}) async-start(f32[32,2,8,128]{3,2,1,0:T(8,128)} %broadcast_in_dim.28), calls=%async_computation | async-start | bytes 524288 | tf_op jit(solution)/shard_map/all_to_all | solution.py:323
  9.0 10.3 %invert.1 = (s32[6144]{0:T(1024)}, s32[48,128]{1,0:T(8,128)}) custom-call(s32[6144]{0:T(1024)} %cell_of_state.1, s32[48,128]{1,0:T(8,128)} %bitcast.7), custom_call_target="tpu_custom_call" | custom-call | flops 10000000 | bytes 30000000 | tf_op jit(solution)/shard_map/invert/pallas_call | solution.py:325
  19.3 0.0 all-to-all-done.shared
  19.3 0.0 copy-start
  19.3 0.7 copy-done
  20.0 25.6 %first_pass.1 = (f32[32,288,128]{2,1,0:T(8,128)}, f32[50,8,128]{2,1,0:T(8,128)}) custom-call(s32[6144]{0:T(1024)} %bitcast.8, s32[6144]{0:T(1024)} %get-tuple-element.10.state_of_cell, f32[192,6144]{1,0:T(8,128)} %x_hbm.1, f32[32,2,8,128]{3,2,1,0:T(8,128)} %copy-done, s32[1,4,2,6144]{3,2,1,0:T(2,128)} %flags.3), custom_call_target="tpu_custom_call" | custom-call | flops 25000000 | bytes 75000000 | tf_op jit(solution)/shard_map/first_pass/pallas_call | solution.py:339
  45.6 0.0 copy-start.1
  45.6 6.1 %all-to-all-start.1 = ((f32[32,288,128]{2,1,0:T(8,128)}), f32[32,288,128]{2,1,0:T(8,128)}, u32[]{:S(2)}, u32[]{:S(2)}) async-start(f32[32,288,128]{2,1,0:T(8,128)} %get-tuple-element.11), calls=%async_computation.1 | async-start | bytes 9437184 | tf_op jit(solution)/shard_map/all_to_all | solution.py:352
  51.7 0.1 iota.32
  51.9 0.0 copy-done.1
  51.9 0.1 broadcast_in_dim.30
  52.0 0.1 broadcast_in_dim.31
  52.1 0.1 iota.28
  52.3 0.9 fusion.extra
  53.2 104.5 %all-to-all-done.1.a_hbm = f32[32,288,128]{2,1,0:T(8,128)} async-done(((f32[32,288,128]{2,1,0:T(8,128)}), f32[32,288,128]{2,1,0:T(8,128)}, u32[]{:S(2)}, u32[]{:S(2)}) %all-to-all-start.1) | async-done | bytes 4718624 | tf_op jit(solution)/shard_map/all_to_all | solution.py:352
  157.7 25.4 %second_pass.1 = f32[192,6144]{1,0:T(8,128)} custom-call(s32[6144]{0:T(1024)} %bitcast.9, s32[6144]{0:T(1024)} %get-tuple-element.10.state_of_cell, s32[1]{0:T(128)} %bitcast.2.place, f32[32,288,128]{2,1,0:T(8,128)} %all-to-all-done.1.a_hbm, f32[50,8,128]{2,1,0:T(8,128)} %get-tuple-element.12.rates, s32[1,4,2,6144]{3,2,1,0:T(2,128)} %flags.3, ...), custom_call_target="tpu_custom_call" | custom-call | flops 25000000 | bytes 75000000 | tf_op jit(solution)/shard_map/second_pass/pallas_call | solution.py:361
  (4 shorter events, 0.0 us)
Async XLA Ops:
  1.7 17.6 %all-to-all-start = ((f32[32,2,8,128]{3,2,1,0:T(8,128)}), f32[32,2,8,128]{3,2,1,0:T(8,128)S(1)}, u32[]{:S(2)}, u32[]{:S(2)}) async-start(f32[32,2,8,128]{3,2,1,0:T(8,128)} %broadcast_in_dim.28), calls=%async_computation | async-start | bytes 524288 | tf_op jit(solution)/shard_map/all_to_all | solution.py:323
  19.3 0.7 copy-start
  45.6 6.3 %copy-start.1 = (f32[1,192]{1,0:T(1,128)S(1)}, f32[1,192]{1,0:T(1,128)}, u32[]{:S(2)}) copy-start(f32[1,192]{1,0:T(1,128)} %param.9) | copy-start | bytes 2308
  45.6 112.2 %all-to-all-start.1 = ((f32[32,288,128]{2,1,0:T(8,128)}), f32[32,288,128]{2,1,0:T(8,128)}, u32[]{:S(2)}, u32[]{:S(2)}) async-start(f32[32,288,128]{2,1,0:T(8,128)} %get-tuple-element.11), calls=%async_computation.1 | async-start | bytes 9437184 | tf_op jit(solution)/shard_map/all_to_all | solution.py:352
